TPU v7x, 512 devices: a whole 4x8x8 slice. The times are simulated.
512 devices in a mesh: day: 32 (over z, x), tile: 16 (over y, core).
Axes of the slice: x: 4, y: 8, z: 8, core: 2. Of those that a mesh axis runs over, the one named last changes fastest.
Arguments:
- causal: bfloat16 [32, 1, 1024, 1024], P('day', None, 'tile'), may hold values from -24 to 24
- acausal_held: bfloat16 [32, 1, 1024, 1024], P('day', None, 'tile'), may hold values from -24 to 24
- fk_bins: int32 [512, 1024], P('day'), may hold values from 0 to 7
- band_gain: float32 [8], replicated, may hold values from 0.1 to 1
Outputs:
- filtered: float32 [1024, 1, 1024], P('day', None, 'tile')
All inputs are finite; a program needn't handle non-finite values.
Results may differ from a plain program's by a relative error of at most 0.0023.
Values may be sent and summed in bfloat16 or wider, within the bound.
No kernel may reach another device: no remote copies, remote signals or barrier semaphores. Data moves between devices by JAX's collectives and lax.ppermute only.
A program may use at most 64 MiB of HBM per device.

v0:
```python
import math

import jax
import jax.numpy as jnp
from jax import lax
from jax.sharding import PartitionSpec as P


def swapped(block, axis, bit):
    count = lax.axis_size(axis)
    route = []
    for low in range(count):
        high = low | 1 << bit
        if high != low and high < count:
            route += [(low, high), (high, low)]
    return lax.ppermute(block, axis, route)


def spectrum_block(data, first, size, lag_count):
    freq = first + lax.iota(jnp.int32, size)
    lags = lax.iota(jnp.int32, lag_count)
    phase = (freq[:, None] * lags[None, :] % lag_count).astype(jnp.float32) * (
        2.0 * math.pi / lag_count
    )
    basis_table = (
        jnp.stack([jnp.cos(phase), -jnp.sin(phase)], axis=1) / math.sqrt(lag_count)
    ).astype(jnp.bfloat16)
    return jnp.einsum("fcl,drl->fcr", basis_table, data, preferred_element_type=jnp.float32)


def spectrum_rows(data, count, lag_count):
    firsts = 128 * lax.iota(jnp.int32, count // 128)

    def one_block(first):
        return spectrum_block(data, first, 128, lag_count)

    blocks = lax.map(one_block, firsts)
    return blocks.reshape(count, 2, data.shape[1])


def wavenumber_filter(lines, gains):
    real_part = lines[:, 0]
    imaginary_part = lines[:, 1]
    count = real_part.shape[-1]
    width = min(256, count)
    scale = 1.0 / math.sqrt(count)
    upper_half = lax.Precision.HIGHEST

    def forward(lower_half, basis_table):
        return jnp.einsum("zhy,yu->zhu", lower_half, basis_table, precision=upper_half)

    def backward(lower_half, basis_table):
        return jnp.einsum("vct,mt->vcm", lower_half, basis_table, precision=upper_half)

    def turn(index, carry):
        back_real, back_imag = carry
        first = index * width
        waves = first + lax.iota(jnp.int32, width)
        recv = lax.iota(jnp.int32, count)
        phase = (recv[:, None] * waves[None, :] % count).astype(jnp.float32) * (
            2.0 * math.pi / count
        )
        cosine_basis = jnp.cos(phase) * scale
        sine_basis = jnp.sin(phase) * scale
        gain_block = lax.dynamic_slice_in_dim(gains, first, width, 1)[:, None, :]
        waveform_real = (
            forward(real_part, cosine_basis) + forward(imaginary_part, sine_basis)
        ) * gain_block
        waveform_imaginary = (
            forward(imaginary_part, cosine_basis) - forward(real_part, sine_basis)
        ) * gain_block
        back_real = (
            back_real
            + backward(waveform_real, cosine_basis)
            - backward(waveform_imaginary, sine_basis)
        )
        back_imag = (
            back_imag
            + backward(waveform_imaginary, cosine_basis)
            + backward(waveform_real, sine_basis)
        )
        return (back_real, back_imag)

    start = (jnp.zeros_like(real_part), jnp.zeros_like(imaginary_part))
    back_real, back_imag = lax.fori_loop(0, count // width, turn, start)
    return jnp.stack([back_real, back_imag], axis=1)


def body(causal, acausal_held, fk_bins, band_gain):
    day_local, shot_count, block_recv, lag_count = causal.shape
    day_devices = lax.axis_size("day")
    tile_devices = lax.axis_size("tile")
    day_total = day_local * day_devices
    freq_count = lag_count // 2
    freq_local = freq_count // day_devices
    row_count = shot_count * block_recv
    top_bit = tile_devices.bit_length() - 2
    causal_data = causal.reshape(day_local, row_count, lag_count)
    inverse_days = 1.0 / day_total
    held_data = acausal_held.reshape(day_local, row_count, lag_count)
    first = spectrum_rows(causal_data, lax.axis_size("day") * freq_local, lag_count)
    second = spectrum_rows(held_data, lax.axis_size("day") * freq_local, lag_count)
    spectra = lax.psum_scatter(
        jnp.stack([first, second], axis=1) * inverse_days, "day", scatter_dimension=0, tiled=True
    )
    mirrored = swapped(spectra[:, 1], "tile", top_bit)
    folded = spectra[:, 0] + mirrored
    folded = folded.reshape(freq_local, 2, shot_count, block_recv)
    line_freq = freq_local // tile_devices
    bins_local = lax.dynamic_slice_in_dim(fk_bins, lax.axis_index("tile") * line_freq, line_freq, 0)
    levels = lax.iota(jnp.int32, band_gain.shape[0])
    gains = jnp.sum(jnp.where(bins_local[:, :, None] == levels, band_gain, 0.0), axis=-1)
    filtered_lines = wavenumber_filter(
        lax.all_to_all(folded, "tile", split_axis=0, concat_axis=3, tiled=True), gains
    )
    returned = lax.all_to_all(filtered_lines, "tile", split_axis=3, concat_axis=0, tiled=True)
    real_flat = returned[:, 0].reshape(freq_local, row_count)
    imag_flat = returned[:, 1].reshape(freq_local, row_count)
    freq_base = lax.axis_index("day") * freq_local
    count = lax.axis_size("day") * (lag_count // day_devices)
    lags = lax.iota(jnp.int32, count)
    freq = freq_base + lax.iota(jnp.int32, freq_local)
    angle = (lags[:, None] * freq[None, :] % lag_count).astype(jnp.float32) * (
        2.0 * math.pi / lag_count
    )
    weight = jnp.where(freq == 0, 1.0, 2.0).astype(jnp.float32)[None, :] / math.sqrt(lag_count)
    inverse_cosine_basis = weight * jnp.cos(angle)
    inverse_sine_basis = -weight * jnp.sin(angle)
    term = jnp.dot(
        inverse_cosine_basis,
        real_flat,
        precision=lax.Precision.HIGHEST,
        preferred_element_type=jnp.float32,
    )
    term = term + jnp.dot(
        inverse_sine_basis,
        imag_flat,
        precision=lax.Precision.HIGHEST,
        preferred_element_type=jnp.float32,
    )
    return lax.psum_scatter(
        term.reshape(count, shot_count, block_recv), "day", scatter_dimension=0, tiled=True
    )


def solution(mesh):
    return jax.shard_map(
        body,
        mesh=mesh,
        in_specs=(P("day", None, "tile", None), P("day", None, "tile", None), P("day", None), P()),
        out_specs=P("day", None, "tile"),
        check_vma=False,
    )
```

profile of v0, /device:TPU:24, one launch (start us, length us, event | category | flops | bytes accessed | tf_op | source)
XLA Modules:
  0.0 657.0 jit_solution(14282304691270742736)
XLA Ops:
  7.5 19.7 %while.42 = (s32[]{:T(128)}, f32[4,128,2,64]{1,0,3,2:T(4,128)S(1)}, s32[4]{0:T(128)S(1)}, bf16[1,64,1024]{2,1,0:T(8,128)(2,1)S(1)}, s32[]{:T(128)}, /*index=5*/s32[]{:T(128)}) while((s32[]{:T(128)}, f32[4,128,2,64]{1,0,3,2:T(4,128)S(1)}, s32[4]{0:T(128)S(1)}, bf16[1,64,1024]{2,1,0:T(8,128)(2,1)S(1)}, s32[]{:T(128)}, ...), condition=%wide.region_2.3_spmd, body=%wide.region_1.2_spmd.sunk | while | flops 36307072 | bytes 2425945 | solution.py:37
  28.2 19.7 %while.43 = (s32[]{:T(128)}, f32[4,128,2,64]{1,0,3,2:T(4,128)S(1)}, s32[4]{0:T(128)S(1)}, bf16[1,64,1024]{2,1,0:T(8,128)(2,1)S(1)}, s32[]{:T(128)}, /*index=5*/s32[]{:T(128)}) while((s32[]{:T(128)}, f32[4,128,2,64]{1,0,3,2:T(4,128)S(1)}, s32[4]{0:T(128)S(1)}, bf16[1,64,1024]{2,1,0:T(8,128)(2,1)S(1)}, s32[]{:T(128)}, ...), condition=%wide.region_4.5_spmd, body=%wide.region_3.4_spmd.sunk | while | flops 36307072 | bytes 2425945 | solution.py:37
  51.4 164.5 %all-reduce.3.cloned.1.call-done = f32[512,2,2,64]{3,2,1,0:T(2,128)} async-done(((f32[512,2,2,64]{3,2,1,0:T(2,128)}), f32[512,2,2,64]{3,2,1,0:T(2,128)}) %all-reduce.3.cloned.1.call-update) | async-done | bytes 524304
  216.6 4.8 collective-permute-start
  221.5 4.8 collective-permute-done
  227.7 7.3 %all-to-all-start = ((f32[16,1,128]{2,1,0:T(1,128)}), f32[16,1,128]{2,1,0:T(1,128)S(1)}, u32[]{:S(2)}, u32[]{:S(2)}) async-start(f32[16,1,128]{2,1,0:T(1,128)} %reshape.395), calls=%async_computation | async-start | bytes 16384 | tf_op jit(solution)/shard_map/all_to_all | solution.py:114
  240.7 169.5 %while.44 = (s32[]{:T(128)}, f32[1,1,1024]{2,1,0:T(1,128)S(1)}, f32[1,1,1024]{2,1,0:T(1,128)S(1)}, f32[1,1,1024]{2,1,0:T(1,128)S(1)}, f32[1,1,1024]{2,1,0:T(1,12...) while((s32[]{:T(128)}, f32[1,1,1024]{2,1,0:T(1,128)S(1)}, ...), condition=%wide.region_7.8_spmd.clone, body=%wide.region_6.7_spmd.clone.sunk | while | flops 56630532 | bytes 75942 | solution.py:85
  261.0 4.5 fusion.174
  269.9 4.5 fusion.176
  274.4 5.0 fusion.179
  279.5 5.1 fusion.180
  284.6 5.1 fusion.177
  289.7 5.1 fusion.178
  308.3 4.5 fusion.176
  312.8 5.0 fusion.179
  317.9 5.1 fusion.180
  323.0 5.1 fusion.177
  328.1 5.1 fusion.178
  337.8 4.5 fusion.174
  346.7 4.5 fusion.176
  351.2 5.0 fusion.179
  356.3 5.1 fusion.180
  361.4 5.1 fusion.177
  366.5 5.1 fusion.178
  376.2 4.5 fusion.174
  385.1 4.5 fusion.176
  389.6 5.0 fusion.179
  394.7 5.1 fusion.180
  399.8 5.1 fusion.177
  404.9 5.1 fusion.178
  413.4 6.5 all-to-all-start.1
  432.3 217.5 %reduce-scatter.2.cloned.1.call-done = f32[32,1,64]{2,1,0:T(1,128)} async-done(((f32[1024,1,64]{2,1,0:T(1,128)}), f32[32,1,64]{2,1,0:T(1,128)}) %reduce-scatter.2.cloned.1.call-update) | async-done | bytes 8208 | tf_op jit(solution)/shard_map/reduce_scatter | solution.py:141
  (109 shorter events, 107.7 us)
Async XLA Ops:
  6.5 44.9 %copy-start = (s32[16,1024]{1,0:T(8,128)S(1)}, s32[16,1024]{1,0:T(8,128)}, u32[]{:S(2)}) copy-start(s32[16,1024]{1,0:T(8,128)} %param.12) | copy-start | bytes 196612
  6.5 209.4 %all-reduce.3.cloned.1.call-start = ((), (), s32[]{:S(2)}) async-start(), calls=%async_computation.4 | async-start | bytes 2097152
  6.5 0.9 copy-start.2
  27.3 0.9 copy-start.3
  216.6 4.8 copy-start.1
  216.6 9.7 %collective-permute-start = (f32[16,2,64]{2,1,0:T(2,128)S(1)}, f32[16,2,64]{2,1,0:T(2,128)S(1)}, u32[]{:S(2)}, u32[]{:S(2)}) collective-permute-start(f32[16,2,64]{2,1,0:T(2,128)S(1)} %dynamic-slice_bitcast_fusion), channel_id=1, source_target_pairs={{0,8},{8,0},{1,9},{9,1},{2,10},{10,2},{3,11},{11,3},{4,12},{12,4},... | collective-permute-start | bytes 24584 | tf_op jit(solution)/shard_map/ppermute | solution.py:16
  227.7 11.7 %all-to-all-start = ((f32[16,1,128]{2,1,0:T(1,128)}), f32[16,1,128]{2,1,0:T(1,128)S(1)}, u32[]{:S(2)}, u32[]{:S(2)}) async-start(f32[16,1,128]{2,1,0:T(1,128)} %reshape.395), calls=%async_computation | async-start | bytes 16384 | tf_op jit(solution)/shard_map/all_to_all | solution.py:114
  413.4 10.9 %all-to-all-start.1 = ((f32[16,1,128]{2,1,0:T(1,128)}), f32[16,1,128]{2,1,0:T(1,128)S(1)}, u32[]{:S(2)}, u32[]{:S(2)}) async-start(f32[16,1,128]{2,1,0:T(1,128)} %reshape.397), calls=%async_computation.1 | async-start | bytes 16384 | tf_op jit(solution)/shard_map/all_to_all | solution.py:116
  419.9 229.9 %reduce-scatter.2.cloned.1.call-start = ((), (), s32[]{:S(2)}) async-start(), calls=%async_computation.3 | async-start | bytes 540672 | tf_op jit(solution)/shard_map/reduce_scatter | solution.py:141
Sparse Core Ops, SparseCore 0:
  49.6 166.2 all-reduce.2
  432.4 217.2 reduce-scatter.1
where the time goes:
time: 663 us; the launch traced here: 657 us
  waiting for transfers between devices  395 us (60%)
  matrix products  161 us (24%)
  other arithmetic  25.6 us (4%)
  local copies, waits for them, and re-layouts  25.5 us (4%)
  starting transfers between devices  18.6 us (3%)
  loops' own time  16.4 us (2%)
  between operations  14.6 us (2%)
    reduce_scatter x1, waiting for transfers between devices, body(): lax.psum_scatter(term.reshape(count, shot_count, block_recv), 'day', scat...  217 us
    unnamed x3, waiting for transfers between devices  165 us
    dot_general x16, matrix products, backward(): jnp.einsum('vct,mt->vcm', lower_half, basis_table, precision=upper_half)  81.5 us
    dot_general x16, matrix products, forward(): jnp.einsum('zhy,yu->zhu', lower_half, basis_table, precision=upper_half)  71.7 us
    cos x8, other arithmetic, spectrum_block(): jnp.cos(phase)  17 us
    another operation x1, loops' own time, wavenumber_filter(): back_real, back_imag = lax.fori_loop(0, count // width, turn, start)  16.1 us
  transfers between devices with their start and end apart: 5, of which 5 were waited for; matrix products, arithmetic and copies ran while one was open for 0% of the time, Pallas kernels for 0%

commit v1 on v0

v1 whole, which is shorter than its diff:
```python
import functools
import math

import jax
import jax.numpy as jnp
import numpy as np
from jax import lax
from jax.experimental import pallas as pl
from jax.experimental.pallas import tpu as pltpu
from jax.sharding import PartitionSpec as P

HIGHEST = lax.Precision.HIGHEST


def lag_basis(freq_count, lag_count, owners):
    freq = np.arange(freq_count)
    phase = (freq[:, None] * np.arange(lag_count)[None, :] % lag_count) * (2.0 * np.pi / lag_count)
    table = np.stack([np.cos(phase), -np.sin(phase)], axis=0) / math.sqrt(lag_count)
    table = table.reshape(2, owners, freq_count // owners, lag_count).transpose(1, 0, 2, 3)
    return table.reshape(2 * freq_count, lag_count).astype(np.float32).astype(jnp.bfloat16)


def halves(real_part, imag_part):
    return np.concatenate([real_part, imag_part], axis=-1).astype(np.float32)


def block_dft(width, sign, scale):
    angle = (np.arange(width)[:, None] * np.arange(width)[None, :] % width) * (2.0 * np.pi / width)
    cosine, sine = np.cos(angle) * scale, sign * np.sin(angle) * scale
    return np.concatenate([halves(cosine, sine), halves(-sine, cosine)], axis=0)


def other_half(value):
    return pltpu.roll(value, value.shape[-1] // 2, value.ndim - 1)


def lag_kernel(table_ref, causal_ref, held_ref, out_ref):
    rows = jnp.concatenate([causal_ref[...], held_ref[...]], axis=0)
    out_ref[...] = lax.dot_general(
        table_ref[...], rows, (((1,), (1,)), ((), ())), preferred_element_type=jnp.float32
    ).astype(out_ref.dtype)


def stack_kernel(scale, parts_ref, out_ref):
    count = parts_ref.shape[0]
    total = parts_ref[0].astype(jnp.float32)
    for day in range(1, count):
        total = total + parts_ref[day].astype(jnp.float32)
    total = total * scale
    half = total.shape[0] // 2
    real_part, imag_part = total[:half], total[half:]
    low = lax.broadcasted_iota(jnp.int32, real_part.shape, 1) < real_part.shape[1] // 2
    causal = jnp.where(low, real_part, other_half(imag_part))
    held = jnp.where(low, other_half(real_part), imag_part)
    for peer in range(out_ref.shape[0]):
        out_ref[peer, :half] = causal
        out_ref[peer, half:] = held


def filter_kernel(
    lines_ref, gains_ref, fore_ref, back_ref, turn_ref, unturn_ref, out_ref, work_ref
):
    blocks = lines_ref.shape[0]
    half = lines_ref.shape[1] // 2
    shape = (half, lines_ref.shape[2])
    low = lax.broadcasted_iota(jnp.int32, shape, 1) < shape[1] // 2
    sign = jnp.where(low, 1.0, -1.0)

    def minus_i(value):
        return other_half(value) * sign

    def rotated(value, power):
        power %= 16
        if power == 0:
            return value
        cosine, sine = math.cos(math.pi * power / 8), math.sin(math.pi * power / 8)
        return value * cosine + minus_i(value) * sine

    def four(a, b, c, d):
        p, m, q, n = a + c, a - c, b + d, minus_i(b - d)
        return p + q, m + n, p - q, m - n

    data = [lines_ref[j, :half] + lines_ref[(j + blocks // 2) % blocks, half:] for j in range(blocks)]
    inner = [four(*(data[4 * a + b] for a in range(4))) for b in range(4)]
    for c in range(4):
        outer = four(*(rotated(inner[b][c], b * c) for b in range(4)))
        for d in range(4):
            q = c + 4 * d
            value = outer[d]
            work_ref[q * half : (q + 1) * half] = (
                value * turn_ref[0, q : q + 1] + other_half(value) * turn_ref[1, q : q + 1]
            )
    wave = jnp.dot(
        work_ref[...], fore_ref[...], precision=HIGHEST, preferred_element_type=jnp.float32
    )
    masked = wave * gains_ref[...]
    work_ref[...] = jnp.dot(
        masked, back_ref[...], precision=HIGHEST, preferred_element_type=jnp.float32
    )
    total = None
    for q in range(blocks):
        value = work_ref[q * half : (q + 1) * half]
        term = value * unturn_ref[0, q : q + 1] + other_half(value) * unturn_ref[1, q : q + 1]
        total = term if total is None else total + term
    for peer in range(out_ref.shape[0]):
        out_ref[peer] = total


def gather_kernel(lines_ref, table_ref, out_ref):
    both = jnp.dot(
        table_ref[...], lines_ref[...], precision=HIGHEST, preferred_element_type=jnp.float32
    )
    half, width = both.shape[0] // 2, both.shape[1] // 2
    out_ref[...] = both[:half, :width] + other_half(both[half:])[:, :width]


def body(causal, acausal_held, fk_bins, band_gain):
    _, _, width, lag_count = causal.shape
    days, tiles = lax.axis_size("day"), lax.axis_size("tile")
    freq_count = lag_count // 2
    freq_local = freq_count // days
    recv_count = width * tiles
    lag_local = lag_count // days
    lanes = 2 * width
    day, tile = lax.axis_index("day"), lax.axis_index("tile")

    steps = 4
    table = jnp.asarray(lag_basis(freq_count, lag_count, days))
    block = 2 * freq_count // steps
    spectra = pl.pallas_call(
        lag_kernel,
        grid=(steps,),
        in_specs=[
            pl.BlockSpec((block, lag_count), lambda s: (s, 0)),
            pl.BlockSpec((width, lag_count), lambda s: (0, 0)),
            pl.BlockSpec((width, lag_count), lambda s: (0, 0)),
        ],
        out_specs=pl.BlockSpec((block, lanes), lambda s: (s, 0)),
        out_shape=jax.ShapeDtypeStruct((2 * freq_count, lanes), jnp.bfloat16),
    )(table, causal.reshape(width, lag_count), acausal_held.reshape(width, lag_count))
    parts = lax.all_to_all(
        spectra.reshape(days, 2 * freq_local, lanes), "day", 0, 0, tiled=True
    )
    stacked = pl.pallas_call(
        functools.partial(stack_kernel, 1.0 / days),
        out_shape=jax.ShapeDtypeStruct((tiles, 2 * freq_local, lanes), jnp.float32),
    )(parts)

    levels = lax.iota(jnp.int32, band_gain.shape[0])
    ordered = fk_bins.reshape(freq_local, width, tiles).transpose(2, 0, 1)
    gains = jnp.sum(jnp.where(ordered[..., None] == levels, band_gain, 0.0), axis=-1)
    gains = jnp.concatenate([gains, gains], axis=-1).reshape(tiles * freq_local, lanes)
    residue = lax.iota(jnp.int32, tiles)
    recv = tile * width + lax.iota(jnp.int32, width)
    angle = (residue[:, None] * recv[None, :] % recv_count).astype(jnp.float32) * (
        2.0 * math.pi / recv_count
    )
    cosine, sine = jnp.cos(angle), jnp.sin(angle)
    unturn = jnp.stack(
        [jnp.concatenate([cosine, cosine], axis=1), jnp.concatenate([-sine, sine], axis=1)]
    )
    lag = day * lag_local + lax.iota(jnp.int32, lag_local)
    freq = lax.iota(jnp.int32, freq_count)
    angle = (lag[:, None] * freq[None, :] % lag_count).astype(jnp.float32) * (
        2.0 * math.pi / lag_count
    )
    weight = jnp.where(freq == 0, 1.0, 2.0).astype(jnp.float32)[None, :] / math.sqrt(lag_count)
    inverse_table = jnp.concatenate([weight * jnp.cos(angle), -weight * jnp.sin(angle)], axis=0)

    scale = 1.0 / math.sqrt(recv_count)
    turn_angle = np.arange(tiles)[:, None] * np.arange(width)[None, :] * (2.0 * np.pi / recv_count)
    turn = np.stack(
        [
            halves(np.cos(turn_angle), np.cos(turn_angle)),
            halves(np.sin(turn_angle), -np.sin(turn_angle)),
        ]
    )
    gathered = lax.all_to_all(stacked, "tile", 0, 0, tiled=True)
    lines = pl.pallas_call(
        filter_kernel,
        out_shape=jax.ShapeDtypeStruct((days, freq_local, lanes), jnp.float32),
        scratch_shapes=[pltpu.VMEM((tiles * freq_local, lanes), jnp.float32)],
    )(
        gathered,
        gains,
        jnp.asarray(block_dft(width, -1.0, scale)),
        jnp.asarray(block_dft(width, 1.0, scale)),
        jnp.asarray(turn),
        unturn,
    )
    returned = lax.all_to_all(lines, "day", 0, 0, tiled=True)
    filtered = pl.pallas_call(
        gather_kernel,
        out_shape=jax.ShapeDtypeStruct((lag_local, width), jnp.float32),
    )(returned.reshape(freq_count, lanes), inverse_table)
    return filtered.reshape(lag_local, 1, width)


def solution(mesh):
    return jax.shard_map(
        body,
        mesh=mesh,
        in_specs=(P("day", None, "tile", None), P("day", None, "tile", None), P("day", None), P()),
        out_specs=P("day", None, "tile"),
        check_vma=False,
    )
```

time: 663 us -> 76.1 us (0.11)
  the two profiles are of different devices: /device:TPU:24 before, /device:TPU:1 now
where the time goes in v1:
time: 76.1 us; the launch traced here: 75.6 us
  waiting for transfers between devices  32.2 us (42%)
  starting transfers between devices  27.3 us (36%)
  Pallas kernels  10.5 us (14%)
  other arithmetic  2.96 us (4%)
  local copies, waits for them, and re-layouts  2.53 us (3%)
    all_to_all x1, starting transfers between devices, body(): lax.all_to_all(spectra.reshape(days, 2 * freq_local, lanes), 'day', 0, 0,...  13.8 us
    all_to_all x1, waiting for transfers between devices, body(): returned = lax.all_to_all(lines, 'day', 0, 0, tiled=True)  11.7 us
    all_to_all x1, waiting for transfers between devices, body(): lax.all_to_all(spectra.reshape(days, 2 * freq_local, lanes), 'day', 0, 0,...  11.3 us
    all_to_all x1, starting transfers between devices, body(): gathered = lax.all_to_all(stacked, 'tile', 0, 0, tiled=True)  9.57 us
    all_to_all x1, waiting for transfers between devices, body(): gathered = lax.all_to_all(stacked, 'tile', 0, 0, tiled=True)  9.24 us
    pallas_call x1, Pallas kernels, body(): pl.pallas_call(lag_kernel, grid=(steps,), in_specs=[pl.BlockSpec((block,...  4.06 us
    all_to_all x1, starting transfers between devices, body(): returned = lax.all_to_all(lines, 'day', 0, 0, tiled=True)  3.87 us
    pallas_call x1, Pallas kernels, body(): pl.pallas_call(filter_kernel, out_shape=jax.ShapeDtypeStruct((days, freq_...  2.74 us
  transfers between devices with their start and end apart: 3, of which 3 were waited for; matrix products, arithmetic and copies ran while one was open for 4% of the time, Pallas kernels for 0%

profile of v1, /device:TPU:1, one launch (start us, length us, event | category | flops | bytes accessed | tf_op | source)
XLA Modules:
  0.0 75.6 jit_solution(14862684210921757176)
XLA Ops:
  0.0 0.0 copy-start.3
  0.0 4.1 %shard_map.82 = bf16[1024,128]{1,0:T(8,128)(2,1)} custom-call(bf16[1024,1024]{1,0:T(8,128)(2,1)} %constant.57.clone.table_ref, bf16[64,1024]{1,0:T(8,128)(2,1)} %bitcast.17, bf16[64,1024]{1,0:T(8,128)(2,1)} %bitcast.18), custom_call_target="tpu_custom_call" | custom-call | tf_op jit(solution)/shard_map/pallas_call | solution.py:130
  4.1 0.0 copy-start.4
  4.1 13.8 %all-to-all-start = ((bf16[32,32,128]{2,1,0:T(8,128)(2,1)}), bf16[32,32,128]{2,1,0:T(8,128)(2,1)S(1)}, u32[]{:S(2)}, u32[]{:S(2)}) async-start(bf16[32,32,128]{2,1,0:T(8,128)(2,1)} %bitcast.14), calls=%async_computation | async-start | bytes 524288 | tf_op jit(solution)/shard_map/all_to_all | solution.py:141
  17.9 11.3 %all-to-all-done.parts_ref = bf16[32,32,128]{2,1,0:T(8,128)(2,1)S(1)} async-done(((bf16[32,32,128]{2,1,0:T(8,128)(2,1)}), bf16[32,32,128]{2,1,0:T(8,128)(2,1)S(1)}, u32[]{:S(2)}, u32[]{:S(2)}) %all-to-all-start) | async-done | bytes 262176 | tf_op jit(solution)/shard_map/all_to_all | solution.py:141
  29.2 0.0 copy-start.2
  29.2 0.7 copy-done.2
  29.9 1.8 %shard_map.83 = f32[16,32,128]{2,1,0:T(8,128)} custom-call(bf16[32,32,128]{2,1,0:T(8,128)(2,1)} %copy-done.2), custom_call_target="tpu_custom_call" | custom-call | tf_op jit(solution)/shard_map/pallas_call | solution.py:144
  31.7 9.6 %all-to-all-start.1 = ((f32[16,32,128]{2,1,0:T(8,128)}), f32[16,32,128]{2,1,0:T(8,128)S(1)}, u32[]{:S(2)}, u32[]{:S(2)}) async-start(f32[16,32,128]{2,1,0:T(8,128)} %shard_map.83), calls=%async_computation.1 | async-start | bytes 524288 | tf_op jit(solution)/shard_map/all_to_all | solution.py:178
  41.3 0.1 fusion.13
  41.4 0.0 copy-done.3
  41.4 0.2 reshape.44
  41.6 0.2 copy.13
  41.8 0.1 maximum_bitcast_fusion
  41.8 0.6 pad_maximum_fusion.2.unturn_ref
  42.5 0.0 copy-done.4
  42.5 0.4 select_reduce_fusion
  42.9 0.8 %pad_maximum_fusion = f32[16,16,128]{2,1,0:T(8,128)} fusion(f32[16,16,64]{2,1,0:T(8,128)S(1)} %select_reduce_fusion), kind=kLoop, calls=%fused_computation.2 | loop fusion | flops 32768 | bytes 196608 | tf_op jit(solution)/shard_map/concatenate | solution.py:152
  43.6 9.2 %all-to-all-done.1.lines_ref = f32[16,32,128]{2,1,0:T(8,128)S(1)} async-done(((f32[16,32,128]{2,1,0:T(8,128)}), f32[16,32,128]{2,1,0:T(8,128)S(1)}, u32[]{:S(2)}, u32[]{:S(2)}) %all-to-all-start.1) | async-done | bytes 262176 | tf_op jit(solution)/shard_map/all_to_all | solution.py:178
  52.9 0.0 copy-start
  52.9 0.7 copy-done
  53.6 2.7 %shard_map.84 = f32[32,16,128]{2,1,0:T(8,128)} custom-call(f32[16,32,128]{2,1,0:T(8,128)} %copy-done, f32[256,128]{1,0:T(8,128)} %bitcast.16, f32[128,128]{1,0:T(8,128)} %constant.58.clone.fore_ref, f32[128,128]{1,0:T(8,128)} %constant.59.clone.back_ref, f32[2,16,128]{2,1,0:T(8,128)} %constant.60.clone.turn_ref, f32[2,16,128]{2,1,0:T(8,128)} %pad_maximum_fusion.2.unturn_ref), custom_call_target="tpu_custom_call" | custom-call | tf_op jit(solution)/shard_map/pallas_call | solution.py:179
  56.3 3.9 %all-to-all-start.2 = ((f32[32,16,128]{2,1,0:T(8,128)}), f32[32,16,128]{2,1,0:T(8,128)S(1)}, u32[]{:S(2)}, u32[]{:S(2)}) async-start(f32[32,16,128]{2,1,0:T(8,128)} %shard_map.84), calls=%async_computation.2 | async-start | bytes 524288 | tf_op jit(solution)/shard_map/all_to_all | solution.py:191
  60.2 0.3 cosine_multiply_fusion
  60.6 0.7 pad_maximum_fusion.1.table_ref
  61.3 11.7 %all-to-all-done.2 = f32[32,16,128]{2,1,0:T(8,128)S(1)} async-done(((f32[32,16,128]{2,1,0:T(8,128)}), f32[32,16,128]{2,1,0:T(8,128)S(1)}, u32[]{:S(2)}, u32[]{:S(2)}) %all-to-all-start.2) | async-done | bytes 262176 | tf_op jit(solution)/shard_map/all_to_all | solution.py:191
  73.0 0.0 copy-start.1
  73.0 0.7 copy-done.1
  73.7 1.9 %shard_map.85 = f32[32,64]{1,0:T(8,128)} custom-call(f32[512,128]{1,0:T(8,128)} %bitcast.15, f32[64,512]{1,0:T(8,128)} %pad_maximum_fusion.1.table_ref), custom_call_target="tpu_custom_call" | custom-call | tf_op jit(solution)/shard_map/pallas_call | solution.py:192
  (3 shorter events, 0.0 us)
Async XLA Ops:
  0.0 41.4 %copy-start.3 = (s32[16,1024]{1,0:T(8,128)S(1)}, s32[16,1024]{1,0:T(8,128)}, u32[]{:S(2)}) copy-start(s32[16,1024]{1,0:T(8,128)} %param.10) | copy-start | bytes 196612
  4.1 38.4 %copy-start.4 = (f32[8]{0:T(128)S(1)}, f32[8]{0:T(128)}, u32[]{:S(2)}) copy-start(f32[8]{0:T(128)} %param.11) | copy-start | bytes 100
  4.1 25.1 %all-to-all-start = ((bf16[32,32,128]{2,1,0:T(8,128)(2,1)}), bf16[32,32,128]{2,1,0:T(8,128)(2,1)S(1)}, u32[]{:S(2)}, u32[]{:S(2)}) async-start(bf16[32,32,128]{2,1,0:T(8,128)(2,1)} %bitcast.14), calls=%async_computation | async-start | bytes 524288 | tf_op jit(solution)/shard_map/all_to_all | solution.py:141
  29.2 0.7 copy-start.2
  31.7 21.2 %all-to-all-start.1 = ((f32[16,32,128]{2,1,0:T(8,128)}), f32[16,32,128]{2,1,0:T(8,128)S(1)}, u32[]{:S(2)}, u32[]{:S(2)}) async-start(f32[16,32,128]{2,1,0:T(8,128)} %shard_map.83), calls=%async_computation.1 | async-start | bytes 524288 | tf_op jit(solution)/shard_map/all_to_all | solution.py:178
  52.9 0.7 copy-start
  56.3 16.7 %all-to-all-start.2 = ((f32[32,16,128]{2,1,0:T(8,128)}), f32[32,16,128]{2,1,0:T(8,128)S(1)}, u32[]{:S(2)}, u32[]{:S(2)}) async-start(f32[32,16,128]{2,1,0:T(8,128)} %shard_map.84), calls=%async_computation.2 | async-start | bytes 524288 | tf_op jit(solution)/shard_map/all_to_all | solution.py:191
  73.0 0.7 copy-start.1

commit v2 on v1

v2 whole, which is shorter than its diff:
```python
import functools
import math

import jax
import jax.numpy as jnp
import numpy as np
from jax import lax
from jax.experimental import pallas as pl
from jax.experimental.pallas import tpu as pltpu
from jax.sharding import Mesh
from jax.sharding import PartitionSpec as P

AXES = ("day", "high", "low", "core")
SCALE = 2.0**46
TINY = 2.0**-125
VMEM = pl.BlockSpec(memory_space=pltpu.VMEM)
HBM = pl.BlockSpec(memory_space=pltpu.HBM)
PARAMS = pltpu.CompilerParams(vmem_limit_bytes=8 * 2**20)


def lag_basis(freq_count, lag_count, owners):
    freq = np.arange(freq_count)
    phase = (freq[:, None] * np.arange(lag_count)[None, :] % lag_count) * (2.0 * np.pi / lag_count)
    table = np.stack([np.cos(phase), -np.sin(phase)], axis=0) / math.sqrt(lag_count)
    table = table[:, :, : lag_count // 2].reshape(2, owners, freq_count // owners, lag_count // 2)
    table = table.transpose(1, 0, 2, 3).reshape(2 * freq_count, lag_count // 2)
    return table.astype(np.float32).astype(jnp.bfloat16)


def halves(real_part, imag_part):
    return np.concatenate([real_part, imag_part], axis=-1).astype(np.float32)


def block_dft(width, sign, scale):
    angle = (np.arange(width)[:, None] * np.arange(width)[None, :] % width) * (2.0 * np.pi / width)
    cosine, sine = np.cos(angle) * scale, sign * np.sin(angle) * scale
    return np.concatenate([halves(cosine, sine), halves(-sine, cosine)], axis=0)


def other_half(value):
    return pltpu.roll(value, value.shape[-1] // 2, value.ndim - 1)


def lag_kernel(
    table_hbm, causal_hbm, held_hbm, out_hbm, table_ref, rows_ref, out_ref, sems, out_sems
):
    pieces = out_sems.shape[0]
    width = causal_hbm.shape[0]
    size = table_ref.shape[0] // pieces
    half = table_ref.shape[1]
    inputs = [
        pltpu.make_async_copy(causal_hbm, rows_ref.at[pl.ds(0, width)], sems.at[pieces]),
        pltpu.make_async_copy(held_hbm, rows_ref.at[pl.ds(width, width)], sems.at[pieces + 1]),
    ]
    tables = [
        pltpu.make_async_copy(
            table_hbm.at[pl.ds(p * size, size)], table_ref.at[pl.ds(p * size, size)], sems.at[p]
        )
        for p in range(pieces)
    ]
    for copy in inputs + tables:
        copy.start()
    for copy in inputs:
        copy.wait()
    rows = rows_ref[...]
    sides = jnp.concatenate([rows[:, :half], rows[:, half:]], axis=0)
    lanes = 2 * width
    odd = lax.broadcasted_iota(jnp.int32, (size, lanes), 0) % 2
    sign = (1 - 2 * odd).astype(jnp.float32)
    outputs = []
    for p in range(pieces):
        tables[p].wait()
        both = lax.dot_general(
            table_ref[p * size : (p + 1) * size],
            sides,
            (((1,), (1,)), ((), ())),
            preferred_element_type=jnp.float32,
        )
        out_ref[p * size : (p + 1) * size] = (both[:, :lanes] + sign * both[:, lanes:]).astype(
            out_ref.dtype
        )
        outputs.append(
            pltpu.make_async_copy(
                out_ref.at[pl.ds(p * size, size)], out_hbm.at[pl.ds(p * size, size)], out_sems.at[p]
            )
        )
        outputs[p].start()
    for copy in outputs:
        copy.wait()


def coded(value):
    value = value * SCALE
    return (value * jnp.abs(value)).astype(jnp.bfloat16)


def decoded(code):
    code = code.astype(jnp.float32)
    return code * lax.rsqrt(jnp.maximum(jnp.abs(code), TINY)) * (1.0 / SCALE)


def split(value):
    high = value.astype(jnp.bfloat16)
    return high, (value - high.astype(jnp.float32)).astype(jnp.bfloat16)


def split_rows(matrix):
    high = matrix.astype(jnp.bfloat16)
    low = (matrix - high.astype(np.float32)).astype(jnp.bfloat16)
    return np.concatenate([high, high, low], axis=0)


def product(value, matrix):
    high, low = split(value)
    return jnp.dot(
        jnp.concatenate([high, low, high], axis=1), matrix, preferred_element_type=jnp.float32
    )


def stack_kernel(scale, parts_ref, out_ref):
    count, pairs = parts_ref.shape[0], parts_ref.shape[1]
    half = parts_ref.shape[2] // 2
    totals = [parts_ref[0, pair].astype(jnp.float32) for pair in range(pairs)]
    for day in range(1, count):
        totals = [totals[pair] + parts_ref[day, pair].astype(jnp.float32) for pair in range(pairs)]
    for pair in range(pairs):
        total = totals[pair] * scale
        real_part, imag_part = total[:half], total[half:]
        low = lax.broadcasted_iota(jnp.int32, real_part.shape, 1) < real_part.shape[1] // 2
        causal = jnp.where(low, real_part, other_half(imag_part))
        held = jnp.where(low, other_half(real_part), imag_part)
        code = coded(jnp.concatenate([causal, held], axis=0))
        for peer in range(out_ref.shape[0]):
            out_ref[peer, pair] = code


def filter_kernel(
    lines_ref, gains_ref, fore_ref, back_ref, turn_ref, unturn_ref, out_ref, work_ref
):
    peers, pairs, half, lanes = lines_ref.shape
    half //= 2
    blocks = peers * pairs
    low = lax.broadcasted_iota(jnp.int32, (half, lanes), 1) < lanes // 2
    sign = jnp.where(low, 1.0, -1.0)

    def minus_i(value):
        return other_half(value) * sign

    def rotated(value, power):
        power %= 16
        if power == 0:
            return value
        cosine, sine = math.cos(math.pi * power / 8), math.sin(math.pi * power / 8)
        return value * cosine + minus_i(value) * sine

    def four(a, b, c, d):
        p, m, q, n = a + c, a - c, b + d, minus_i(b - d)
        return p + q, m + n, p - q, m - n

    data = []
    value = decoded(lines_ref[...])
    for block in range(blocks):
        high, pair, core = block // (2 * pairs), block // 2 % pairs, block % 2
        peer = 2 * high + core
        data.append(value[peer, pair, :half] + value[(peer + peers // 2) % peers, pair, half:])
    inner = [four(*(data[4 * a + b] for a in range(4))) for b in range(4)]
    for c in range(4):
        outer = four(*(rotated(inner[b][c], b * c) for b in range(4)))
        for d in range(4):
            q = c + 4 * d
            value = outer[d]
            work_ref[q * half : (q + 1) * half] = (
                value * turn_ref[0, q : q + 1] + other_half(value) * turn_ref[1, q : q + 1]
            )
    wave = product(work_ref[...], fore_ref[...])
    work_ref[...] = product(wave * gains_ref[...], back_ref[...])
    for pair in range(pairs):
        total = None
        for q in range(blocks):
            value = work_ref[q * half : (q + 1) * half]
            term = value * unturn_ref[pair, 0, q : q + 1] + other_half(value) * unturn_ref[
                pair, 1, q : q + 1
            ]
            total = term if total is None else total + term
        code = coded(total)
        for day in range(out_ref.shape[0] // pairs):
            out_ref[day * pairs + pair] = code


def gather_kernel(codes_ref, table_ref, out_ref):
    owners, freqs, lanes = codes_ref.shape
    lines = decoded(codes_ref[...]).reshape(owners * freqs, lanes)
    line_high, line_low = split(lines)
    table_high, table_low = split(table_ref[...])
    rows, width = table_high.shape[0] // 2, lanes // 2
    both = jnp.dot(
        jnp.concatenate([table_high, table_low], axis=0),
        line_high,
        preferred_element_type=jnp.float32,
    )
    both = both[: 2 * rows] + both[2 * rows :]
    both = both + jnp.dot(table_high, line_low, preferred_element_type=jnp.float32)
    out_ref[...] = both[:rows, :width] + other_half(both[rows:])[:, :width]


def body(causal, acausal_held, fk_bins, band_gain):
    _, _, width, lag_count = causal.shape
    days, highs, pairs, cores = (lax.axis_size(name) for name in AXES)
    tiles = highs * pairs * cores
    owners = days * pairs
    freq_count = lag_count // 2
    freq_local = freq_count // owners
    recv_count = width * tiles
    lag_local = lag_count // days
    lanes = 2 * width
    day, high, pair, core = (lax.axis_index(name) for name in AXES)

    table = jnp.asarray(lag_basis(freq_count, lag_count, owners))
    pieces = 2
    spectra = pl.pallas_call(
        lag_kernel,
        in_specs=[HBM] * 3,
        out_specs=HBM,
        out_shape=jax.ShapeDtypeStruct((2 * freq_count, lanes), jnp.bfloat16),
        scratch_shapes=[
            pltpu.VMEM((2 * freq_count, lag_count // 2), jnp.bfloat16),
            pltpu.VMEM((lanes, lag_count), jnp.bfloat16),
            pltpu.VMEM((2 * freq_count, lanes), jnp.bfloat16),
            pltpu.SemaphoreType.DMA((pieces + 2,)),
            pltpu.SemaphoreType.DMA((pieces,)),
        ],
    )(table, causal.reshape(width, lag_count), acausal_held.reshape(width, lag_count))
    parts = lax.all_to_all(
        spectra.reshape(owners, 2 * freq_local, lanes), ("day", "low"), 0, 0, tiled=True
    )

    levels = lax.iota(jnp.int32, band_gain.shape[0])
    own_bins = lax.dynamic_slice_in_dim(fk_bins, pair * freq_local, freq_local, 0)
    ordered = own_bins.reshape(freq_local, width, tiles).transpose(2, 0, 1)
    gains = jnp.sum(jnp.where(ordered[..., None] == levels, band_gain, 0.0), axis=-1)
    gains = jnp.concatenate([gains, gains], axis=-1).reshape(tiles * freq_local, lanes)
    residue = lax.iota(jnp.int32, tiles)
    own_blocks = (high * pairs + lax.iota(jnp.int32, pairs)) * cores + core
    recv = own_blocks[:, None] * width + lax.iota(jnp.int32, width)[None, :]
    angle = (residue[None, :, None] * recv[:, None, :] % recv_count).astype(jnp.float32) * (
        2.0 * math.pi / recv_count
    )
    cosine, sine = jnp.cos(angle), jnp.sin(angle)
    unturn = jnp.stack(
        [jnp.concatenate([cosine, cosine], axis=2), jnp.concatenate([-sine, sine], axis=2)],
        axis=1,
    )
    lag = day * lag_local + lax.iota(jnp.int32, lag_local)
    freq = lax.iota(jnp.int32, freq_count)
    angle = (lag[:, None] * freq[None, :] % lag_count).astype(jnp.float32) * (
        2.0 * math.pi / lag_count
    )
    weight = jnp.where(freq == 0, 1.0, 2.0).astype(jnp.float32)[None, :] / math.sqrt(lag_count)
    inverse_table = jnp.concatenate([weight * jnp.cos(angle), -weight * jnp.sin(angle)], axis=0)
    parts, gains, unturn, inverse_table = lax.optimization_barrier(
        (parts, gains, unturn, inverse_table)
    )

    stacked = pl.pallas_call(
        functools.partial(stack_kernel, 1.0 / days),
        in_specs=[VMEM],
        out_specs=VMEM,
        compiler_params=PARAMS,
        out_shape=jax.ShapeDtypeStruct(
            (highs * cores, pairs, 2 * freq_local, lanes), jnp.bfloat16
        ),
    )(parts.reshape(days, pairs, 2 * freq_local, lanes))
    scale = 1.0 / math.sqrt(recv_count)
    turn_angle = np.arange(tiles)[:, None] * np.arange(width)[None, :] * (2.0 * np.pi / recv_count)
    turn = np.stack(
        [
            halves(np.cos(turn_angle), np.cos(turn_angle)),
            halves(np.sin(turn_angle), -np.sin(turn_angle)),
        ]
    )
    gathered = lax.all_to_all(stacked, ("high", "core"), 0, 0, tiled=True)
    lines = pl.pallas_call(
        filter_kernel,
        in_specs=[VMEM] * 6,
        out_specs=VMEM,
        compiler_params=PARAMS,
        out_shape=jax.ShapeDtypeStruct((owners, freq_local, lanes), jnp.bfloat16),
        scratch_shapes=[pltpu.VMEM((tiles * freq_local, lanes), jnp.float32)],
    )(
        gathered,
        gains,
        jnp.asarray(split_rows(block_dft(width, -1.0, scale))),
        jnp.asarray(split_rows(block_dft(width, 1.0, scale))),
        jnp.asarray(turn),
        unturn,
    )
    returned = lax.all_to_all(
        lines, ("day", "low"), 0, 0, tiled=True
    )
    filtered = pl.pallas_call(
        gather_kernel,
        in_specs=[VMEM] * 2,
        out_specs=VMEM,
        compiler_params=PARAMS,
        out_shape=jax.ShapeDtypeStruct((lag_local, width), jnp.float32),
    )(returned, inverse_table)
    return filtered.reshape(lag_local, 1, width)


def solution(mesh):
    days, tiles = mesh.devices.shape
    split = Mesh(mesh.devices.reshape(days, tiles // 4, 2, 2), AXES)
    tile = ("high", "low", "core")
    return jax.shard_map(
        body,
        mesh=split,
        in_specs=(P("day", None, tile, None), P("day", None, tile, None), P("day", None), P()),
        out_specs=P("day", None, tile),
        check_vma=False,
    )
```

time: 76.1 us -> 62.2 us (0.82)
  the two profiles are of different devices: /device:TPU:1 before, /device:TPU:8 now
where the time goes in v2:
time: 62.2 us; the launch traced here: 61.9 us
  blocking collectives  29.9 us (48%)
  starting transfers between devices  14.8 us (24%)
  waiting for transfers between devices  10.7 us (17%)
  Pallas kernels  4.54 us (7%)
  other arithmetic  0.94 us (2%)
  local copies, waits for them, and re-layouts  0.92 us (1%)
    all_to_all x1, blocking collectives, body(): returned = lax.all_to_all(lines, ('day', 'low'), 0, 0, tiled=True)  15.5 us
    all_to_all x1, starting transfers between devices, body(): lax.all_to_all(spectra.reshape(owners, 2 * freq_local, lanes), ('day', 'l...  14.8 us
    all_to_all x1, blocking collectives, body(): gathered = lax.all_to_all(stacked, ('high', 'core'), 0, 0, tiled=True)  14.5 us
    all_to_all x1, waiting for transfers between devices, body(): lax.all_to_all(spectra.reshape(owners, 2 * freq_local, lanes), ('day', 'l...  10.7 us
    pallas_call x1, Pallas kernels, body(): pl.pallas_call(lag_kernel, in_specs=[HBM] * 3, out_specs=HBM, out_shape=j...  2.82 us
  transfers between devices with their start and end apart: 1, of which 1 were waited for; matrix products, arithmetic and copies ran while one was open for 2% of the time, Pallas kernels for 0%

profile of v2, /device:TPU:8, one launch (start us, length us, event | category | flops | bytes accessed | tf_op | source)
XLA Modules:
  0.0 61.9 jit_solution(16689225939804363617)
XLA Ops:
  0.0 0.0 copy-start
  0.0 2.8 %shard_map.82 = bf16[1024,128]{1,0:T(8,128)(2,1)} custom-call(bf16[1024,512]{1,0:T(8,128)(2,1)} %constant.73.clone.table_hbm, bf16[64,1024]{1,0:T(8,128)(2,1)} %bitcast.19, bf16[64,1024]{1,0:T(8,128)(2,1)} %bitcast.20), custom_call_target="tpu_custom_call" | custom-call | tf_op jit(solution)/shard_map/pallas_call | solution.py:220
  2.8 14.8 %all-to-all-start = ((bf16[64,16,128]{2,1,0:T(8,128)(2,1)}), bf16[64,16,128]{2,1,0:T(8,128)(2,1)S(1)}, u32[]{:S(2)}, u32[]{:S(2)}) async-start(bf16[64,16,128]{2,1,0:T(8,128)(2,1)} %bitcast.18), calls=%async_computation | async-start | bytes 524288 | tf_op jit(solution)/shard_map/all_to_all | solution.py:233
  17.7 0.0 copy-done
  17.7 0.1 reshape.65
  17.8 0.1 copy.14
  18.0 0.1 iota_add_fusion
  18.0 0.1 fusion.13
  18.1 0.0 copy-start.4
  18.1 0.6 %copy-done.4 = f32[8]{0:T(128)S(1)} copy-done((f32[8]{0:T(128)S(1)}, f32[8]{0:T(128)}, u32[]{:S(2)}) %copy-start.4) | copy-done | bytes 56
  18.8 0.2 select_reduce_fusion
  19.0 0.1 maximum_bitcast_fusion.1
  19.1 0.1 maximum_bitcast_fusion.gains_ref
  19.2 0.3 cosine_multiply_fusion
  19.6 10.7 %all-to-all-done = bf16[64,16,128]{2,1,0:T(8,128)(2,1)S(1)} async-done(((bf16[64,16,128]{2,1,0:T(8,128)(2,1)}), bf16[64,16,128]{2,1,0:T(8,128)(2,1)S(1)}, u32[]{:S(2)}, u32[]{:S(2)}) %all-to-all-start) | async-done | bytes 262176 | tf_op jit(solution)/shard_map/all_to_all | solution.py:233
  30.2 0.0 copy-start.2
  30.2 0.1 shard_map.83
  30.4 0.0 copy-start.1
  30.4 0.0 copy-start.3
  30.4 14.5 %all_to_all.15.lines_ref = bf16[8,2,16,128]{3,2,1,0:T(8,128)(2,1)S(1)} all-to-all(bf16[8,2,16,128]{3,2,1,0:T(8,128)(2,1)S(1)} %shard_map.83), channel_id=1, replica_groups=mesh['day'=32,'high'=4,'low'=2,'core'=2] {'high','core'}, dimensions={0} | all-to-all | bytes 131072 | tf_op jit(solution)/shard_map/all_to_all | solution.py:281
  44.9 0.0 copy-done.2
  44.9 0.0 copy-done.1
  44.9 0.0 copy-done.3
  44.9 0.7 %shard_map.84 = bf16[64,8,128]{2,1,0:T(8,128)(2,1)S(1)} custom-call(bf16[8,2,16,128]{3,2,1,0:T(8,128)(2,1)S(1)} %all_to_all.15.lines_ref, f32[128,128]{1,0:T(8,128)S(1)} %maximum_bitcast_fusion.gains_ref, bf16[384,128]{1,0:T(8,128)(2,1)S(1)} %copy-done.1, bf16[384,128]{1,0:T(8,128)(2,1)S(1)} %copy-done.2, f32[2,16,128]{2,1,0:T(8,128)S(1)} %copy-done.3, ...), custom_call_target="tpu_custom_call" | custom-call | tf_op jit(solution)/shard_map/pallas_call | solution.py:282
  45.5 15.5 %all_to_all.16.codes_ref = bf16[64,8,128]{2,1,0:T(8,128)(2,1)S(1)} all-to-all(bf16[64,8,128]{2,1,0:T(8,128)(2,1)S(1)} %shard_map.84), channel_id=1, replica_groups=mesh['day'=32,'high'=4,'low'=2,'core'=2] {'day','low'}, dimensions={0} | all-to-all | bytes 262144 | tf_op jit(solution)/shard_map/all_to_all | solution.py:297
  61.0 0.9 %shard_map.85 = f32[32,64]{1,0:T(8,128)} custom-call(bf16[64,8,128]{2,1,0:T(8,128)(2,1)S(1)} %all_to_all.16.codes_ref, f32[64,512]{1,0:T(8,128)S(1)} %pad_maximum_fusion.table_ref), custom_call_target="tpu_custom_call" | custom-call | tf_op jit(solution)/shard_map/pallas_call | solution.py:300
  (6 shorter events, 0.0 us)
Async XLA Ops:
  0.0 17.7 %copy-start = (s32[16,1024]{1,0:T(8,128)S(1)}, s32[16,1024]{1,0:T(8,128)}, u32[]{:S(2)}) copy-start(s32[16,1024]{1,0:T(8,128)} %param.10) | copy-start | bytes 196612
  2.8 27.4 %all-to-all-start = ((bf16[64,16,128]{2,1,0:T(8,128)(2,1)}), bf16[64,16,128]{2,1,0:T(8,128)(2,1)S(1)}, u32[]{:S(2)}, u32[]{:S(2)}) async-start(bf16[64,16,128]{2,1,0:T(8,128)(2,1)} %bitcast.18), calls=%async_computation | async-start | bytes 524288 | tf_op jit(solution)/shard_map/all_to_all | solution.py:233
  18.1 0.7 %copy-start.4 = (f32[8]{0:T(128)S(1)}, f32[8]{0:T(128)}, u32[]{:S(2)}) copy-start(f32[8]{0:T(128)} %param.11) | copy-start | bytes 100
  30.2 14.6 %copy-start.2 = (bf16[384,128]{1,0:T(8,128)(2,1)S(1)}, bf16[384,128]{1,0:T(8,128)(2,1)}, u32[]{:S(2)}) copy-start(bf16[384,128]{1,0:T(8,128)(2,1)} %constant.75.clone.back_ref) | copy-start | bytes 294916
  30.4 14.5 %copy-start.1 = (bf16[384,128]{1,0:T(8,128)(2,1)S(1)}, bf16[384,128]{1,0:T(8,128)(2,1)}, u32[]{:S(2)}) copy-start(bf16[384,128]{1,0:T(8,128)(2,1)} %constant.74.clone.fore_ref) | copy-start | bytes 294916
  30.4 14.5 %copy-start.3 = (f32[2,16,128]{2,1,0:T(8,128)S(1)}, f32[2,16,128]{2,1,0:T(8,128)}, u32[]{:S(2)}) copy-start(f32[2,16,128]{2,1,0:T(8,128)} %constant.76.clone.turn_ref) | copy-start | bytes 49156

commit v3 on v2

--- a/solution.py
+++ b/solution.py
@@ -10,7 +10,7 @@
 from jax.sharding import Mesh
 from jax.sharding import PartitionSpec as P
 
-AXES = ("day", "high", "low", "core")
+AXES = ("z", "x", "high", "low", "core")
 SCALE = 2.0**46
 TINY = 2.0**-125
 VMEM = pl.BlockSpec(memory_space=pltpu.VMEM)
@@ -161,8 +161,9 @@
     value = decoded(lines_ref[...])
     for block in range(blocks):
         high, pair, core = block // (2 * pairs), block // 2 % pairs, block % 2
-        peer = 2 * high + core
-        data.append(value[peer, pair, :half] + value[(peer + peers // 2) % peers, pair, half:])
+        highs = peers // 2
+        peer, other = core * highs + high, core * highs + (high + highs // 2) % highs
+        data.append(value[peer, pair, :half] + value[other, pair, half:])
     inner = [four(*(data[4 * a + b] for a in range(4))) for b in range(4)]
     for c in range(4):
         outer = four(*(rotated(inner[b][c], b * c) for b in range(4)))
@@ -189,23 +190,25 @@
 
 def gather_kernel(codes_ref, table_ref, out_ref):
     owners, freqs, lanes = codes_ref.shape
-    lines = decoded(codes_ref[...]).reshape(owners * freqs, lanes)
-    line_high, line_low = split(lines)
-    table_high, table_low = split(table_ref[...])
-    rows, width = table_high.shape[0] // 2, lanes // 2
-    both = jnp.dot(
-        jnp.concatenate([table_high, table_low], axis=0),
-        line_high,
-        preferred_element_type=jnp.float32,
-    )
-    both = both[: 2 * rows] + both[2 * rows :]
-    both = both + jnp.dot(table_high, line_low, preferred_element_type=jnp.float32)
-    out_ref[...] = both[:rows, :width] + other_half(both[rows:])[:, :width]
+    rows, width = table_ref.shape[0] // 4, lanes // 2
+    chunks = 2
+    size = owners // chunks
+    total = None
+    for c in range(chunks):
+        lines = decoded(codes_ref[c * size : (c + 1) * size]).reshape(size * freqs, lanes)
+        line_high, line_low = split(lines)
+        table = table_ref[:, c * size * freqs : (c + 1) * size * freqs]
+        both = jnp.dot(table, line_high, preferred_element_type=jnp.float32)
+        both = both[: 2 * rows] + both[2 * rows :]
+        both = both + jnp.dot(table[: 2 * rows], line_low, preferred_element_type=jnp.float32)
+        total = both if total is None else total + both
+    out_ref[...] = total[:rows, :width] + other_half(total[rows:])[:, :width]
 
 
 def body(causal, acausal_held, fk_bins, band_gain):
     _, _, width, lag_count = causal.shape
-    days, highs, pairs, cores = (lax.axis_size(name) for name in AXES)
+    depth, breadth, highs, pairs, cores = (lax.axis_size(name) for name in AXES)
+    days = depth * breadth
     tiles = highs * pairs * cores
     owners = days * pairs
     freq_count = lag_count // 2
@@ -213,10 +216,11 @@
     recv_count = width * tiles
     lag_local = lag_count // days
     lanes = 2 * width
-    day, high, pair, core = (lax.axis_index(name) for name in AXES)
+    z, x, high, pair, core = (lax.axis_index(name) for name in AXES)
+    day = z * breadth + x
 
     table = jnp.asarray(lag_basis(freq_count, lag_count, owners))
-    pieces = 2
+    pieces = 1
     spectra = pl.pallas_call(
         lag_kernel,
         in_specs=[HBM] * 3,
@@ -231,7 +235,7 @@
         ],
     )(table, causal.reshape(width, lag_count), acausal_held.reshape(width, lag_count))
     parts = lax.all_to_all(
-        spectra.reshape(owners, 2 * freq_local, lanes), ("day", "low"), 0, 0, tiled=True
+        spectra.reshape(owners, 2 * freq_local, lanes), ("z", "x", "low"), 0, 0, tiled=True
     )
 
     levels = lax.iota(jnp.int32, band_gain.shape[0])
@@ -251,12 +255,16 @@
         axis=1,
     )
     lag = day * lag_local + lax.iota(jnp.int32, lag_local)
-    freq = lax.iota(jnp.int32, freq_count)
+    freq = np.arange(freq_count, dtype=np.int32).reshape(depth, breadth, -1)
+    freq = jnp.asarray(freq.transpose(1, 0, 2).reshape(-1))
     angle = (lag[:, None] * freq[None, :] % lag_count).astype(jnp.float32) * (
         2.0 * math.pi / lag_count
     )
     weight = jnp.where(freq == 0, 1.0, 2.0).astype(jnp.float32)[None, :] / math.sqrt(lag_count)
     inverse_table = jnp.concatenate([weight * jnp.cos(angle), -weight * jnp.sin(angle)], axis=0)
+    table_high = lax.reduce_precision(inverse_table, 8, 7)
+    inverse_table = jnp.concatenate([table_high, inverse_table - table_high], axis=0)
+    inverse_table = inverse_table.astype(jnp.bfloat16)
     parts, gains, unturn, inverse_table = lax.optimization_barrier(
         (parts, gains, unturn, inverse_table)
     )
@@ -278,7 +286,7 @@
             halves(np.sin(turn_angle), -np.sin(turn_angle)),
         ]
     )
-    gathered = lax.all_to_all(stacked, ("high", "core"), 0, 0, tiled=True)
+    gathered = lax.all_to_all(stacked, ("core", "high"), 0, 0, tiled=True)
     lines = pl.pallas_call(
         filter_kernel,
         in_specs=[VMEM] * 6,
@@ -295,7 +303,7 @@
         unturn,
     )
     returned = lax.all_to_all(
-        lines, ("day", "low"), 0, 0, tiled=True
+        lines, ("x", "z", "low"), 0, 0, tiled=True
     )
     filtered = pl.pallas_call(
         gather_kernel,
@@ -309,12 +317,12 @@
 
 def solution(mesh):
     days, tiles = mesh.devices.shape
-    split = Mesh(mesh.devices.reshape(days, tiles // 4, 2, 2), AXES)
-    tile = ("high", "low", "core")
+    split = Mesh(mesh.devices.reshape(days // 4, 4, tiles // 2, 1, 2), AXES)
+    day, tile = ("z", "x"), ("high", "low", "core")
     return jax.shard_map(
         body,
         mesh=split,
-        in_specs=(P("day", None, tile, None), P("day", None, tile, None), P("day", None), P()),
-        out_specs=P("day", None, tile),
+        in_specs=(P(day, None, tile, None), P(day, None, tile, None), P(day, None), P()),
+        out_specs=P(day, None, tile),
         check_vma=False,
     )

time: 62.2 us -> 60.7 us (0.976)
  starting transfers between devices: 14.8 us -> 13.3 us
  local copies, waits for them, and re-layouts: 0.92 us -> 1.57 us
    all_to_all x1, starting transfers between devices: 14.8 us -> 13.3 us  [body(): lax.all_to_all(spectra.reshape(owners, 2 * freq_local, lanes), ('z', 'x',...]
where the time goes in v3:
time: 60.7 us; the launch traced here: 60.4 us
  blocking collectives  29.8 us (49%)
  starting transfers between devices  13.3 us (22%)
  waiting for transfers between devices  10.1 us (17%)
  Pallas kernels  4.31 us (7%)
  local copies, waits for them, and re-layouts  1.57 us (3%)
  other arithmetic  1.04 us (2%)
    all_to_all x1, blocking collectives, body(): gathered = lax.all_to_all(stacked, ('core', 'high'), 0, 0, tiled=True)  15.7 us
    all_to_all x1, blocking collectives, body(): returned = lax.all_to_all(lines, ('x', 'z', 'low'), 0, 0, tiled=True)  14.2 us
    all_to_all x1, starting transfers between devices, body(): lax.all_to_all(spectra.reshape(owners, 2 * freq_local, lanes), ('z', 'x',...  13.3 us
    all_to_all x1, waiting for transfers between devices, body(): lax.all_to_all(spectra.reshape(owners, 2 * freq_local, lanes), ('z', 'x',...  10.1 us
    pallas_call x1, Pallas kernels, body(): pl.pallas_call(lag_kernel, in_specs=[HBM] * 3, out_specs=HBM, out_shape=j...  2.57 us
  transfers between devices with their start and end apart: 1, of which 1 were waited for; matrix products, arithmetic and copies ran while one was open for 2% of the time, Pallas kernels for 0%

profile of v3, /device:TPU:8, one launch (start us, length us, event | category | flops | bytes accessed | tf_op | source)
XLA Modules:
  0.0 60.4 jit_solution(4889666735763739431)
XLA Ops:
  0.0 2.6 %shard_map.91 = bf16[1024,128]{1,0:T(8,128)(2,1)} custom-call(bf16[1024,512]{1,0:T(8,128)(2,1)} %constant.78.clone.table_hbm, bf16[64,1024]{1,0:T(8,128)(2,1)} %bitcast.17, bf16[64,1024]{1,0:T(8,128)(2,1)} %bitcast.18), custom_call_target="tpu_custom_call" | custom-call | tf_op jit(solution)/shard_map/pallas_call | solution.py:224
  2.6 0.0 copy-start.3
  2.6 13.3 %all-to-all-start = ((bf16[32,32,128]{2,1,0:T(8,128)(2,1)}), bf16[32,32,128]{2,1,0:T(8,128)(2,1)S(1)}, u32[]{:S(2)}, u32[]{:S(2)}) async-start(bf16[32,32,128]{2,1,0:T(8,128)(2,1)} %bitcast.16), calls=%async_computation | async-start | bytes 524288 | tf_op jit(solution)/shard_map/all_to_all | solution.py:237
  15.9 0.1 fusion.11
  16.0 0.0 copy-done.3
  16.0 0.2 reshape.192
  16.2 0.0 copy-start.7
  16.2 0.2 copy.14
  16.4 0.5 copy-done.7
  16.9 0.4 select_reduce_fusion
  17.3 0.1 pad_maximum_fusion
  17.4 0.0 copy-start.6
  17.4 0.1 maximum_bitcast_fusion
  17.5 0.0 copy-start.5
  17.5 0.0 copy-start.4
  17.5 0.6 copy-done.6
  18.1 0.1 copy-done.5
  18.2 0.0 copy-done.4
  18.2 0.3 cosine_multiply_fusion
  18.6 10.1 %all-to-all-done = bf16[32,32,128]{2,1,0:T(8,128)(2,1)S(1)} async-done(((bf16[32,32,128]{2,1,0:T(8,128)(2,1)}), bf16[32,32,128]{2,1,0:T(8,128)(2,1)S(1)}, u32[]{:S(2)}, u32[]{:S(2)}) %all-to-all-start) | async-done | bytes 262176 | tf_op jit(solution)/shard_map/all_to_all | solution.py:237
  28.7 0.1 shard_map.92
  28.9 0.0 copy-start
  28.9 0.0 copy-start.1
  28.9 0.0 copy-start.2
  28.9 15.7 %all_to_all.15.lines_ref = bf16[16,1,32,128]{3,2,1,0:T(8,128)(2,1)S(1)} all-to-all(bf16[16,1,32,128]{3,2,1,0:T(8,128)(2,1)S(1)} %shard_map.92), channel_id=1, replica_groups=mesh['z'=8,'x'=4,'high'=8,'low'=1,'core'=2] {'core','high'}, dimensions={0} | all-to-all | bytes 262144 | tf_op jit(solution)/shard_map/all_to_all | solution.py:289
  44.6 0.0 copy-done
  44.6 0.0 copy-done.1
  44.6 0.0 copy-done.2
  44.6 0.7 %shard_map.93 = bf16[32,16,128]{2,1,0:T(8,128)(2,1)S(1)} custom-call(bf16[16,1,32,128]{3,2,1,0:T(8,128)(2,1)S(1)} %all_to_all.15.lines_ref, f32[256,128]{1,0:T(8,128)S(1)} %bitcast.14, bf16[384,128]{1,0:T(8,128)(2,1)S(1)} %copy-done, bf16[384,128]{1,0:T(8,128)(2,1)S(1)} %copy-done.1, f32[2,16,128]{2,1,0:T(8,128)S(1)} %copy-done.2, ...), custom_call_target="tpu_custom_call" | custom-call | tf_op jit(solution)/shard_map/pallas_call | solution.py:290
  45.3 14.2 %all_to_all.16.codes_ref = bf16[32,16,128]{2,1,0:T(8,128)(2,1)S(1)} all-to-all(bf16[32,16,128]{2,1,0:T(8,128)(2,1)S(1)} %shard_map.93), channel_id=1, replica_groups=mesh['z'=8,'x'=4,'high'=8,'low'=1,'core'=2] {'x','z','low'}, dimensions={0} | all-to-all | bytes 262144 | tf_op jit(solution)/shard_map/all_to_all | solution.py:305
  59.4 0.9 %shard_map.94 = f32[32,64]{1,0:T(8,128)} custom-call(bf16[32,16,128]{2,1,0:T(8,128)(2,1)S(1)} %all_to_all.16.codes_ref, bf16[128,512]{1,0:T(8,128)(2,1)S(1)} %pad_maximum_fusion.2.table_ref), custom_call_target="tpu_custom_call" | custom-call | tf_op jit(solution)/shard_map/pallas_call | solution.py:308
  (5 shorter events, 0.0 us)
Async XLA Ops:
  2.6 13.4 %copy-start.3 = (s32[16,1024]{1,0:T(8,128)S(1)}, s32[16,1024]{1,0:T(8,128)}, u32[]{:S(2)}) copy-start(s32[16,1024]{1,0:T(8,128)} %param.11) | copy-start | bytes 196612
  2.6 26.1 %all-to-all-start = ((bf16[32,32,128]{2,1,0:T(8,128)(2,1)}), bf16[32,32,128]{2,1,0:T(8,128)(2,1)S(1)}, u32[]{:S(2)}, u32[]{:S(2)}) async-start(bf16[32,32,128]{2,1,0:T(8,128)(2,1)} %bitcast.16), calls=%async_computation | async-start | bytes 524288 | tf_op jit(solution)/shard_map/all_to_all | solution.py:237
  16.2 0.7 %copy-start.7 = (f32[8]{0:T(128)S(1)}, f32[8]{0:T(128)}, u32[]{:S(2)}) copy-start(f32[8]{0:T(128)} %param.12) | copy-start | bytes 100
  17.4 0.7 %copy-start.6 = (f32[512]{0:T(512)S(1)}, f32[512]{0:T(512)}, u32[]{:S(2)}) copy-start(f32[512]{0:T(512)} %constant.89) | copy-start | bytes 6148
  17.5 0.7 %copy-start.5 = (f32[512]{0:T(512)S(1)}, f32[512]{0:T(512)}, u32[]{:S(2)}) copy-start(f32[512]{0:T(512)} %constant.88) | copy-start | bytes 6148
  17.5 0.7 %copy-start.4 = (s32[512]{0:T(512)S(1)}, s32[512]{0:T(512)}, u32[]{:S(2)}) copy-start(s32[512]{0:T(512)} %constant.79.clone) | copy-start | bytes 6148
  28.9 15.7 %copy-start = (bf16[384,128]{1,0:T(8,128)(2,1)S(1)}, bf16[384,128]{1,0:T(8,128)(2,1)}, u32[]{:S(2)}) copy-start(bf16[384,128]{1,0:T(8,128)(2,1)} %constant.80.clone.fore_ref) | copy-start | bytes 294916
  28.9 15.7 %copy-start.1 = (bf16[384,128]{1,0:T(8,128)(2,1)S(1)}, bf16[384,128]{1,0:T(8,128)(2,1)}, u32[]{:S(2)}) copy-start(bf16[384,128]{1,0:T(8,128)(2,1)} %constant.81.clone.back_ref) | copy-start | bytes 294916
  28.9 15.7 %copy-start.2 = (f32[2,16,128]{2,1,0:T(8,128)S(1)}, f32[2,16,128]{2,1,0:T(8,128)}, u32[]{:S(2)}) copy-start(f32[2,16,128]{2,1,0:T(8,128)} %constant.82.clone.turn_ref) | copy-start | bytes 49156

commit v4 on v3

--- a/solution.py
+++ b/solution.py
@@ -42,9 +42,9 @@
 
 
 def lag_kernel(
-    table_hbm, causal_hbm, held_hbm, out_hbm, table_ref, rows_ref, out_ref, sems, out_sems
+    table_hbm, causal_hbm, held_hbm, out_ref, table_ref, rows_ref, sems
 ):
-    pieces = out_sems.shape[0]
+    pieces = sems.shape[0] - 2
     width = causal_hbm.shape[0]
     size = table_ref.shape[0] // pieces
     half = table_ref.shape[1]
@@ -67,7 +67,6 @@
     lanes = 2 * width
     odd = lax.broadcasted_iota(jnp.int32, (size, lanes), 0) % 2
     sign = (1 - 2 * odd).astype(jnp.float32)
-    outputs = []
     for p in range(pieces):
         tables[p].wait()
         both = lax.dot_general(
@@ -79,14 +78,6 @@
         out_ref[p * size : (p + 1) * size] = (both[:, :lanes] + sign * both[:, lanes:]).astype(
             out_ref.dtype
         )
-        outputs.append(
-            pltpu.make_async_copy(
-                out_ref.at[pl.ds(p * size, size)], out_hbm.at[pl.ds(p * size, size)], out_sems.at[p]
-            )
-        )
-        outputs[p].start()
-    for copy in outputs:
-        copy.wait()
 
 
 def coded(value):
@@ -224,16 +215,24 @@
     spectra = pl.pallas_call(
         lag_kernel,
         in_specs=[HBM] * 3,
-        out_specs=HBM,
-        out_shape=jax.ShapeDtypeStruct((2 * freq_count, lanes), jnp.bfloat16),
+        out_specs=VMEM,
+        compiler_params=PARAMS,
+        out_shape=pltpu.VMEM((2 * freq_count, lanes), jnp.bfloat16),
         scratch_shapes=[
             pltpu.VMEM((2 * freq_count, lag_count // 2), jnp.bfloat16),
             pltpu.VMEM((lanes, lag_count), jnp.bfloat16),
-            pltpu.VMEM((2 * freq_count, lanes), jnp.bfloat16),
             pltpu.SemaphoreType.DMA((pieces + 2,)),
-            pltpu.SemaphoreType.DMA((pieces,)),
         ],
-    )(table, causal.reshape(width, lag_count), acausal_held.reshape(width, lag_count))
+    )(
+        *(
+            pltpu.with_memory_space_constraint(operand, pltpu.HBM)
+            for operand in (
+                table,
+                causal.reshape(width, lag_count),
+                acausal_held.reshape(width, lag_count),
+            )
+        )
+    )
     parts = lax.all_to_all(
         spectra.reshape(owners, 2 * freq_local, lanes), ("z", "x", "low"), 0, 0, tiled=True
     )

time: 60.7 us -> 60.7 us (level)
  no operation moved by 1% of the time
where the time goes in v4:
time: 60.7 us; the launch traced here: 60.4 us
  blocking collectives  29.8 us (49%)
  starting transfers between devices  13.3 us (22%)
  waiting for transfers between devices  10.1 us (17%)
  Pallas kernels  4.3 us (7%)
  local copies, waits for them, and re-layouts  1.57 us (3%)
  other arithmetic  1.04 us (2%)
    all_to_all x1, blocking collectives, body(): gathered = lax.all_to_all(stacked, ('core', 'high'), 0, 0, tiled=True)  15.7 us
    all_to_all x1, blocking collectives, body(): returned = lax.all_to_all(lines, ('x', 'z', 'low'), 0, 0, tiled=True)  14.2 us
    all_to_all x1, starting transfers between devices, body(): lax.all_to_all(spectra.reshape(owners, 2 * freq_local, lanes), ('z', 'x',...  13.3 us
    all_to_all x1, waiting for transfers between devices, body(): lax.all_to_all(spectra.reshape(owners, 2 * freq_local, lanes), ('z', 'x',...  10.1 us
    pallas_call x1, Pallas kernels, body(): pl.pallas_call(lag_kernel, in_specs=[HBM] * 3, out_specs=VMEM, compiler_p...  2.56 us
  transfers between devices with their start and end apart: 1, of which 1 were waited for; matrix products, arithmetic and copies ran while one was open for 2% of the time, Pallas kernels for 0%

profile of v4, /device:TPU:8, one launch (start us, length us, event | category | flops | bytes accessed | tf_op | source)
XLA Modules:
  0.0 60.4 jit_solution(3074773017689729084)
XLA Ops:
  0.0 2.6 %shard_map.91 = bf16[1024,128]{1,0:T(8,128)(2,1)} custom-call(bf16[1024,512]{1,0:T(8,128)(2,1)} %constant.78.clone.table_hbm, bf16[64,1024]{1,0:T(8,128)(2,1)} %bitcast.16, bf16[64,1024]{1,0:T(8,128)(2,1)} %bitcast.17), custom_call_target="tpu_custom_call" | custom-call | tf_op jit(solution)/shard_map/pallas_call | solution.py:215
  2.6 0.0 copy-start.3
  2.6 13.3 %all-to-all-start = ((bf16[32,32,128]{2,1,0:T(8,128)(2,1)}), bf16[32,32,128]{2,1,0:T(8,128)(2,1)S(1)}, u32[]{:S(2)}, u32[]{:S(2)}) async-start(bf16[32,32,128]{2,1,0:T(8,128)(2,1)} %bitcast.2), calls=%async_computation | async-start | bytes 524288 | tf_op jit(solution)/shard_map/all_to_all | solution.py:236
  15.9 0.1 fusion.11
  16.0 0.0 copy-done.3
  16.0 0.2 reshape.192
  16.2 0.0 copy-start.7
  16.2 0.2 copy.14
  16.4 0.5 copy-done.7
  16.9 0.4 select_reduce_fusion
  17.3 0.1 pad_maximum_fusion
  17.4 0.0 copy-start.6
  17.4 0.1 maximum_bitcast_fusion
  17.5 0.0 copy-start.5
  17.5 0.0 copy-start.4
  17.5 0.6 copy-done.6
  18.1 0.1 copy-done.5
  18.2 0.0 copy-done.4
  18.2 0.3 cosine_multiply_fusion
  18.6 10.1 %all-to-all-done = bf16[32,32,128]{2,1,0:T(8,128)(2,1)S(1)} async-done(((bf16[32,32,128]{2,1,0:T(8,128)(2,1)}), bf16[32,32,128]{2,1,0:T(8,128)(2,1)S(1)}, u32[]{:S(2)}, u32[]{:S(2)}) %all-to-all-start) | async-done | bytes 262176 | tf_op jit(solution)/shard_map/all_to_all | solution.py:236
  28.7 0.1 shard_map.92
  28.9 0.0 copy-start
  28.9 0.0 copy-start.1
  28.9 0.0 copy-start.2
  28.9 15.7 %all_to_all.15.lines_ref = bf16[16,1,32,128]{3,2,1,0:T(8,128)(2,1)S(1)} all-to-all(bf16[16,1,32,128]{3,2,1,0:T(8,128)(2,1)S(1)} %shard_map.92), channel_id=1, replica_groups=mesh['z'=8,'x'=4,'high'=8,'low'=1,'core'=2] {'core','high'}, dimensions={0} | all-to-all | bytes 262144 | tf_op jit(solution)/shard_map/all_to_all | solution.py:288
  44.6 0.0 copy-done
  44.6 0.0 copy-done.1
  44.6 0.0 copy-done.2
  44.6 0.7 %shard_map.93 = bf16[32,16,128]{2,1,0:T(8,128)(2,1)S(1)} custom-call(bf16[16,1,32,128]{3,2,1,0:T(8,128)(2,1)S(1)} %all_to_all.15.lines_ref, f32[256,128]{1,0:T(8,128)S(1)} %bitcast.14, bf16[384,128]{1,0:T(8,128)(2,1)S(1)} %copy-done, bf16[384,128]{1,0:T(8,128)(2,1)S(1)} %copy-done.1, f32[2,16,128]{2,1,0:T(8,128)S(1)} %copy-done.2, ...), custom_call_target="tpu_custom_call" | custom-call | tf_op jit(solution)/shard_map/pallas_call | solution.py:289
  45.3 14.2 %all_to_all.16.codes_ref = bf16[32,16,128]{2,1,0:T(8,128)(2,1)S(1)} all-to-all(bf16[32,16,128]{2,1,0:T(8,128)(2,1)S(1)} %shard_map.93), channel_id=1, replica_groups=mesh['z'=8,'x'=4,'high'=8,'low'=1,'core'=2] {'x','z','low'}, dimensions={0} | all-to-all | bytes 262144 | tf_op jit(solution)/shard_map/all_to_all | solution.py:304
  59.4 0.9 %shard_map.94 = f32[32,64]{1,0:T(8,128)} custom-call(bf16[32,16,128]{2,1,0:T(8,128)(2,1)S(1)} %all_to_all.16.codes_ref, bf16[128,512]{1,0:T(8,128)(2,1)S(1)} %pad_maximum_fusion.2.table_ref), custom_call_target="tpu_custom_call" | custom-call | tf_op jit(solution)/shard_map/pallas_call | solution.py:307
  (5 shorter events, 0.0 us)
Async XLA Ops:
  2.6 13.4 %copy-start.3 = (s32[16,1024]{1,0:T(8,128)S(1)}, s32[16,1024]{1,0:T(8,128)}, u32[]{:S(2)}) copy-start(s32[16,1024]{1,0:T(8,128)} %param.11) | copy-start | bytes 196612
  2.6 26.1 %all-to-all-start = ((bf16[32,32,128]{2,1,0:T(8,128)(2,1)}), bf16[32,32,128]{2,1,0:T(8,128)(2,1)S(1)}, u32[]{:S(2)}, u32[]{:S(2)}) async-start(bf16[32,32,128]{2,1,0:T(8,128)(2,1)} %bitcast.2), calls=%async_computation | async-start | bytes 524288 | tf_op jit(solution)/shard_map/all_to_all | solution.py:236
  16.2 0.7 %copy-start.7 = (f32[8]{0:T(128)S(1)}, f32[8]{0:T(128)}, u32[]{:S(2)}) copy-start(f32[8]{0:T(128)} %param.12) | copy-start | bytes 100
  17.4 0.7 %copy-start.6 = (f32[512]{0:T(512)S(1)}, f32[512]{0:T(512)}, u32[]{:S(2)}) copy-start(f32[512]{0:T(512)} %constant.89) | copy-start | bytes 6148
  17.5 0.7 %copy-start.5 = (f32[512]{0:T(512)S(1)}, f32[512]{0:T(512)}, u32[]{:S(2)}) copy-start(f32[512]{0:T(512)} %constant.88) | copy-start | bytes 6148
  17.5 0.7 %copy-start.4 = (s32[512]{0:T(512)S(1)}, s32[512]{0:T(512)}, u32[]{:S(2)}) copy-start(s32[512]{0:T(512)} %constant.79.clone) | copy-start | bytes 6148
  28.9 15.7 %copy-start = (bf16[384,128]{1,0:T(8,128)(2,1)S(1)}, bf16[384,128]{1,0:T(8,128)(2,1)}, u32[]{:S(2)}) copy-start(bf16[384,128]{1,0:T(8,128)(2,1)} %constant.80.clone.fore_ref) | copy-start | bytes 294916
  28.9 15.7 %copy-start.1 = (bf16[384,128]{1,0:T(8,128)(2,1)S(1)}, bf16[384,128]{1,0:T(8,128)(2,1)}, u32[]{:S(2)}) copy-start(bf16[384,128]{1,0:T(8,128)(2,1)} %constant.81.clone.back_ref) | copy-start | bytes 294916
  28.9 15.7 %copy-start.2 = (f32[2,16,128]{2,1,0:T(8,128)S(1)}, f32[2,16,128]{2,1,0:T(8,128)}, u32[]{:S(2)}) copy-start(f32[2,16,128]{2,1,0:T(8,128)} %constant.82.clone.turn_ref) | copy-start | bytes 49156

commit v5 on v4

--- a/solution.py
+++ b/solution.py
@@ -75,9 +75,7 @@
             (((1,), (1,)), ((), ())),
             preferred_element_type=jnp.float32,
         )
-        out_ref[p * size : (p + 1) * size] = (both[:, :lanes] + sign * both[:, lanes:]).astype(
-            out_ref.dtype
-        )
+        out_ref[p * size : (p + 1) * size] = coded(both[:, :lanes] + sign * both[:, lanes:])
 
 
 def coded(value):
@@ -111,9 +109,9 @@
 def stack_kernel(scale, parts_ref, out_ref):
     count, pairs = parts_ref.shape[0], parts_ref.shape[1]
     half = parts_ref.shape[2] // 2
-    totals = [parts_ref[0, pair].astype(jnp.float32) for pair in range(pairs)]
+    totals = [decoded(parts_ref[0, pair]) for pair in range(pairs)]
     for day in range(1, count):
-        totals = [totals[pair] + parts_ref[day, pair].astype(jnp.float32) for pair in range(pairs)]
+        totals = [totals[pair] + decoded(parts_ref[day, pair]) for pair in range(pairs)]
     for pair in range(pairs):
         total = totals[pair] * scale
         real_part, imag_part = total[:half], total[half:]

time: 60.7 us -> 60.8 us (level)
  no operation moved by 1% of the time
where the time goes in v5:
time: 60.8 us; the launch traced here: 60.4 us
  blocking collectives  29.8 us (49%)
  starting transfers between devices  13.3 us (22%)
  waiting for transfers between devices  10.1 us (17%)
  Pallas kernels  4.38 us (7%)
  local copies, waits for them, and re-layouts  1.56 us (3%)
  other arithmetic  1.04 us (2%)
    all_to_all x1, blocking collectives, body(): gathered = lax.all_to_all(stacked, ('core', 'high'), 0, 0, tiled=True)  15.7 us
    all_to_all x1, blocking collectives, body(): returned = lax.all_to_all(lines, ('x', 'z', 'low'), 0, 0, tiled=True)  14.2 us
    all_to_all x1, starting transfers between devices, body(): lax.all_to_all(spectra.reshape(owners, 2 * freq_local, lanes), ('z', 'x',...  13.3 us
    all_to_all x1, waiting for transfers between devices, body(): lax.all_to_all(spectra.reshape(owners, 2 * freq_local, lanes), ('z', 'x',...  10.1 us
    pallas_call x1, Pallas kernels, body(): pl.pallas_call(lag_kernel, in_specs=[HBM] * 3, out_specs=VMEM, compiler_p...  2.57 us
  transfers between devices with their start and end apart: 1, of which 1 were waited for; matrix products, arithmetic and copies ran while one was open for 2% of the time, Pallas kernels for 0%

profile of v5, /device:TPU:8, one launch (start us, length us, event | category | flops | bytes accessed | tf_op | source)
XLA Modules:
  0.0 60.4 jit_solution(17491639560191342241)
XLA Ops:
  0.0 2.6 %shard_map.91 = bf16[1024,128]{1,0:T(8,128)(2,1)} custom-call(bf16[1024,512]{1,0:T(8,128)(2,1)} %constant.78.clone.table_hbm, bf16[64,1024]{1,0:T(8,128)(2,1)} %bitcast.16, bf16[64,1024]{1,0:T(8,128)(2,1)} %bitcast.17), custom_call_target="tpu_custom_call" | custom-call | tf_op jit(solution)/shard_map/pallas_call | solution.py:213
  2.6 0.0 copy-start.3
  2.6 13.3 %all-to-all-start = ((bf16[32,32,128]{2,1,0:T(8,128)(2,1)}), bf16[32,32,128]{2,1,0:T(8,128)(2,1)S(1)}, u32[]{:S(2)}, u32[]{:S(2)}) async-start(bf16[32,32,128]{2,1,0:T(8,128)(2,1)} %bitcast.2), calls=%async_computation | async-start | bytes 524288 | tf_op jit(solution)/shard_map/all_to_all | solution.py:234
  15.9 0.1 fusion.11
  16.0 0.0 copy-done.3
  16.0 0.2 reshape.192
  16.2 0.0 copy-start.7
  16.2 0.2 copy.14
  16.4 0.5 copy-done.7
  16.9 0.4 select_reduce_fusion
  17.3 0.1 pad_maximum_fusion
  17.4 0.0 copy-start.6
  17.4 0.1 maximum_bitcast_fusion
  17.5 0.0 copy-start.5
  17.5 0.0 copy-start.4
  17.5 0.6 copy-done.6
  18.1 0.1 copy-done.5
  18.2 0.0 copy-done.4
  18.2 0.3 cosine_multiply_fusion
  18.6 10.1 %all-to-all-done = bf16[32,32,128]{2,1,0:T(8,128)(2,1)S(1)} async-done(((bf16[32,32,128]{2,1,0:T(8,128)(2,1)}), bf16[32,32,128]{2,1,0:T(8,128)(2,1)S(1)}, u32[]{:S(2)}, u32[]{:S(2)}) %all-to-all-start) | async-done | bytes 262176 | tf_op jit(solution)/shard_map/all_to_all | solution.py:234
  28.7 0.2 shard_map.92
  28.9 0.0 copy-start
  28.9 0.0 copy-start.1
  28.9 0.0 copy-start.2
  29.0 15.7 %all_to_all.15.lines_ref = bf16[16,1,32,128]{3,2,1,0:T(8,128)(2,1)S(1)} all-to-all(bf16[16,1,32,128]{3,2,1,0:T(8,128)(2,1)S(1)} %shard_map.92), channel_id=1, replica_groups=mesh['z'=8,'x'=4,'high'=8,'low'=1,'core'=2] {'core','high'}, dimensions={0} | all-to-all | bytes 262144 | tf_op jit(solution)/shard_map/all_to_all | solution.py:286
  44.6 0.0 copy-done
  44.6 0.0 copy-done.1
  44.6 0.0 copy-done.2
  44.6 0.7 %shard_map.93 = bf16[32,16,128]{2,1,0:T(8,128)(2,1)S(1)} custom-call(bf16[16,1,32,128]{3,2,1,0:T(8,128)(2,1)S(1)} %all_to_all.15.lines_ref, f32[256,128]{1,0:T(8,128)S(1)} %bitcast.14, bf16[384,128]{1,0:T(8,128)(2,1)S(1)} %copy-done, bf16[384,128]{1,0:T(8,128)(2,1)S(1)} %copy-done.1, f32[2,16,128]{2,1,0:T(8,128)S(1)} %copy-done.2, ...), custom_call_target="tpu_custom_call" | custom-call | tf_op jit(solution)/shard_map/pallas_call | solution.py:287
  45.3 14.2 %all_to_all.16.codes_ref = bf16[32,16,128]{2,1,0:T(8,128)(2,1)S(1)} all-to-all(bf16[32,16,128]{2,1,0:T(8,128)(2,1)S(1)} %shard_map.93), channel_id=1, replica_groups=mesh['z'=8,'x'=4,'high'=8,'low'=1,'core'=2] {'x','z','low'}, dimensions={0} | all-to-all | bytes 262144 | tf_op jit(solution)/shard_map/all_to_all | solution.py:302
  59.5 0.9 %shard_map.94 = f32[32,64]{1,0:T(8,128)} custom-call(bf16[32,16,128]{2,1,0:T(8,128)(2,1)S(1)} %all_to_all.16.codes_ref, bf16[128,512]{1,0:T(8,128)(2,1)S(1)} %pad_maximum_fusion.2.table_ref), custom_call_target="tpu_custom_call" | custom-call | tf_op jit(solution)/shard_map/pallas_call | solution.py:305
  (5 shorter events, 0.0 us)
Async XLA Ops:
  2.6 13.4 %copy-start.3 = (s32[16,1024]{1,0:T(8,128)S(1)}, s32[16,1024]{1,0:T(8,128)}, u32[]{:S(2)}) copy-start(s32[16,1024]{1,0:T(8,128)} %param.11) | copy-start | bytes 196612
  2.6 26.1 %all-to-all-start = ((bf16[32,32,128]{2,1,0:T(8,128)(2,1)}), bf16[32,32,128]{2,1,0:T(8,128)(2,1)S(1)}, u32[]{:S(2)}, u32[]{:S(2)}) async-start(bf16[32,32,128]{2,1,0:T(8,128)(2,1)} %bitcast.2), calls=%async_computation | async-start | bytes 524288 | tf_op jit(solution)/shard_map/all_to_all | solution.py:234
  16.2 0.7 %copy-start.7 = (f32[8]{0:T(128)S(1)}, f32[8]{0:T(128)}, u32[]{:S(2)}) copy-start(f32[8]{0:T(128)} %param.12) | copy-start | bytes 100
  17.4 0.7 %copy-start.6 = (f32[512]{0:T(512)S(1)}, f32[512]{0:T(512)}, u32[]{:S(2)}) copy-start(f32[512]{0:T(512)} %constant.89) | copy-start | bytes 6148
  17.5 0.7 %copy-start.5 = (f32[512]{0:T(512)S(1)}, f32[512]{0:T(512)}, u32[]{:S(2)}) copy-start(f32[512]{0:T(512)} %constant.88) | copy-start | bytes 6148
  17.5 0.7 %copy-start.4 = (s32[512]{0:T(512)S(1)}, s32[512]{0:T(512)}, u32[]{:S(2)}) copy-start(s32[512]{0:T(512)} %constant.79.clone) | copy-start | bytes 6148
  28.9 15.7 %copy-start = (bf16[384,128]{1,0:T(8,128)(2,1)S(1)}, bf16[384,128]{1,0:T(8,128)(2,1)}, u32[]{:S(2)}) copy-start(bf16[384,128]{1,0:T(8,128)(2,1)} %constant.80.clone.fore_ref) | copy-start | bytes 294916
  28.9 15.7 %copy-start.1 = (bf16[384,128]{1,0:T(8,128)(2,1)S(1)}, bf16[384,128]{1,0:T(8,128)(2,1)}, u32[]{:S(2)}) copy-start(bf16[384,128]{1,0:T(8,128)(2,1)} %constant.81.clone.back_ref) | copy-start | bytes 294916
  28.9 15.7 %copy-start.2 = (f32[2,16,128]{2,1,0:T(8,128)S(1)}, f32[2,16,128]{2,1,0:T(8,128)}, u32[]{:S(2)}) copy-start(f32[2,16,128]{2,1,0:T(8,128)} %constant.82.clone.turn_ref) | copy-start | bytes 49156

commit v6 on v5

--- a/solution.py
+++ b/solution.py
@@ -18,12 +18,12 @@
 PARAMS = pltpu.CompilerParams(vmem_limit_bytes=8 * 2**20)
 
 
-def lag_basis(freq_count, lag_count, owners):
+def lag_basis(freq_count, lag_count, depth, breadth, pairs):
     freq = np.arange(freq_count)
     phase = (freq[:, None] * np.arange(lag_count)[None, :] % lag_count) * (2.0 * np.pi / lag_count)
     table = np.stack([np.cos(phase), -np.sin(phase)], axis=0) / math.sqrt(lag_count)
-    table = table[:, :, : lag_count // 2].reshape(2, owners, freq_count // owners, lag_count // 2)
-    table = table.transpose(1, 0, 2, 3).reshape(2 * freq_count, lag_count // 2)
+    table = table[:, :, : lag_count // 2].reshape(2, depth, breadth, pairs, -1, lag_count // 2)
+    table = table.transpose(2, 1, 3, 0, 4, 5).reshape(2 * freq_count, lag_count // 2)
     return table.astype(np.float32).astype(jnp.bfloat16)
 
 
@@ -208,7 +208,7 @@
     z, x, high, pair, core = (lax.axis_index(name) for name in AXES)
     day = z * breadth + x
 
-    table = jnp.asarray(lag_basis(freq_count, lag_count, owners))
+    table = jnp.asarray(lag_basis(freq_count, lag_count, depth, breadth, pairs))
     pieces = 1
     spectra = pl.pallas_call(
         lag_kernel,
@@ -232,7 +232,7 @@
         )
     )
     parts = lax.all_to_all(
-        spectra.reshape(owners, 2 * freq_local, lanes), ("z", "x", "low"), 0, 0, tiled=True
+        spectra.reshape(owners, 2 * freq_local, lanes), ("x", "z", "low"), 0, 0, tiled=True
     )
 
     levels = lax.iota(jnp.int32, band_gain.shape[0])

time: 60.8 us -> 60.8 us (level)
  no operation moved by 1% of the time
where the time goes in v6:
time: 60.8 us; the launch traced here: 60.5 us
  blocking collectives  30.3 us (50%)
  starting transfers between devices  13.3 us (22%)
  waiting for transfers between devices  9.77 us (16%)
  Pallas kernels  4.38 us (7%)
  local copies, waits for them, and re-layouts  1.56 us (3%)
  other arithmetic  1.04 us (2%)
    all_to_all x1, blocking collectives, body(): gathered = lax.all_to_all(stacked, ('core', 'high'), 0, 0, tiled=True)  15.7 us
    all_to_all x1, blocking collectives, body(): returned = lax.all_to_all(lines, ('x', 'z', 'low'), 0, 0, tiled=True)  14.6 us
    all_to_all x1, starting transfers between devices, body(): lax.all_to_all(spectra.reshape(owners, 2 * freq_local, lanes), ('x', 'z',...  13.3 us
    all_to_all x1, waiting for transfers between devices, body(): lax.all_to_all(spectra.reshape(owners, 2 * freq_local, lanes), ('x', 'z',...  9.77 us
    pallas_call x1, Pallas kernels, body(): pl.pallas_call(lag_kernel, in_specs=[HBM] * 3, out_specs=VMEM, compiler_p...  2.57 us
  transfers between devices with their start and end apart: 1, of which 1 were waited for; matrix products, arithmetic and copies ran while one was open for 2% of the time, Pallas kernels for 0%

profile of v6, /device:TPU:8, one launch (start us, length us, event | category | flops | bytes accessed | tf_op | source)
XLA Modules:
  0.0 60.5 jit_solution(7801943826963549574)
XLA Ops:
  0.0 2.6 %shard_map.91 = bf16[1024,128]{1,0:T(8,128)(2,1)} custom-call(bf16[1024,512]{1,0:T(8,128)(2,1)} %constant.78.clone.table_hbm, bf16[64,1024]{1,0:T(8,128)(2,1)} %bitcast.16, bf16[64,1024]{1,0:T(8,128)(2,1)} %bitcast.17), custom_call_target="tpu_custom_call" | custom-call | tf_op jit(solution)/shard_map/pallas_call | solution.py:213
  2.6 0.0 copy-start.3
  2.6 13.3 %all-to-all-start = ((bf16[32,32,128]{2,1,0:T(8,128)(2,1)}), bf16[32,32,128]{2,1,0:T(8,128)(2,1)S(1)}, u32[]{:S(2)}, u32[]{:S(2)}) async-start(bf16[32,32,128]{2,1,0:T(8,128)(2,1)} %bitcast.2), calls=%async_computation | async-start | bytes 524288 | tf_op jit(solution)/shard_map/all_to_all | solution.py:234
  15.9 0.1 fusion.11
  16.0 0.0 copy-done.3
  16.0 0.2 reshape.192
  16.2 0.0 copy-start.7
  16.2 0.2 copy.14
  16.4 0.5 copy-done.7
  16.9 0.4 select_reduce_fusion
  17.3 0.1 pad_maximum_fusion
  17.4 0.0 copy-start.6
  17.4 0.1 maximum_bitcast_fusion
  17.5 0.0 copy-start.5
  17.5 0.0 copy-start.4
  17.5 0.6 copy-done.6
  18.1 0.1 copy-done.5
  18.2 0.0 copy-done.4
  18.2 0.3 cosine_multiply_fusion
  18.6 9.8 %all-to-all-done = bf16[32,32,128]{2,1,0:T(8,128)(2,1)S(1)} async-done(((bf16[32,32,128]{2,1,0:T(8,128)(2,1)}), bf16[32,32,128]{2,1,0:T(8,128)(2,1)S(1)}, u32[]{:S(2)}, u32[]{:S(2)}) %all-to-all-start) | async-done | bytes 262176 | tf_op jit(solution)/shard_map/all_to_all | solution.py:234
  28.4 0.2 shard_map.92
  28.6 0.0 copy-start
  28.6 0.0 copy-start.1
  28.6 0.0 copy-start.2
  28.6 15.7 %all_to_all.15.lines_ref = bf16[16,1,32,128]{3,2,1,0:T(8,128)(2,1)S(1)} all-to-all(bf16[16,1,32,128]{3,2,1,0:T(8,128)(2,1)S(1)} %shard_map.92), channel_id=1, replica_groups=mesh['z'=8,'x'=4,'high'=8,'low'=1,'core'=2] {'core','high'}, dimensions={0} | all-to-all | bytes 262144 | tf_op jit(solution)/shard_map/all_to_all | solution.py:286
  44.2 0.0 copy-done
  44.2 0.0 copy-done.1
  44.3 0.0 copy-done.2
  44.3 0.7 %shard_map.93 = bf16[32,16,128]{2,1,0:T(8,128)(2,1)S(1)} custom-call(bf16[16,1,32,128]{3,2,1,0:T(8,128)(2,1)S(1)} %all_to_all.15.lines_ref, f32[256,128]{1,0:T(8,128)S(1)} %bitcast.14, bf16[384,128]{1,0:T(8,128)(2,1)S(1)} %copy-done, bf16[384,128]{1,0:T(8,128)(2,1)S(1)} %copy-done.1, f32[2,16,128]{2,1,0:T(8,128)S(1)} %copy-done.2, ...), custom_call_target="tpu_custom_call" | custom-call | tf_op jit(solution)/shard_map/pallas_call | solution.py:287
  45.0 14.6 %all_to_all.16.codes_ref = bf16[32,16,128]{2,1,0:T(8,128)(2,1)S(1)} all-to-all(bf16[32,16,128]{2,1,0:T(8,128)(2,1)S(1)} %shard_map.93), channel_id=1, replica_groups=mesh['z'=8,'x'=4,'high'=8,'low'=1,'core'=2] {'x','z','low'}, dimensions={0} | all-to-all | bytes 262144 | tf_op jit(solution)/shard_map/all_to_all | solution.py:302
  59.6 0.9 %shard_map.94 = f32[32,64]{1,0:T(8,128)} custom-call(bf16[32,16,128]{2,1,0:T(8,128)(2,1)S(1)} %all_to_all.16.codes_ref, bf16[128,512]{1,0:T(8,128)(2,1)S(1)} %pad_maximum_fusion.2.table_ref), custom_call_target="tpu_custom_call" | custom-call | tf_op jit(solution)/shard_map/pallas_call | solution.py:305
  (5 shorter events, 0.0 us)
Async XLA Ops:
  2.6 13.4 %copy-start.3 = (s32[16,1024]{1,0:T(8,128)S(1)}, s32[16,1024]{1,0:T(8,128)}, u32[]{:S(2)}) copy-start(s32[16,1024]{1,0:T(8,128)} %param.11) | copy-start | bytes 196612
  2.6 25.8 %all-to-all-start = ((bf16[32,32,128]{2,1,0:T(8,128)(2,1)}), bf16[32,32,128]{2,1,0:T(8,128)(2,1)S(1)}, u32[]{:S(2)}, u32[]{:S(2)}) async-start(bf16[32,32,128]{2,1,0:T(8,128)(2,1)} %bitcast.2), calls=%async_computation | async-start | bytes 524288 | tf_op jit(solution)/shard_map/all_to_all | solution.py:234
  16.2 0.7 %copy-start.7 = (f32[8]{0:T(128)S(1)}, f32[8]{0:T(128)}, u32[]{:S(2)}) copy-start(f32[8]{0:T(128)} %param.12) | copy-start | bytes 100
  17.4 0.7 %copy-start.6 = (f32[512]{0:T(512)S(1)}, f32[512]{0:T(512)}, u32[]{:S(2)}) copy-start(f32[512]{0:T(512)} %constant.89) | copy-start | bytes 6148
  17.5 0.7 %copy-start.5 = (f32[512]{0:T(512)S(1)}, f32[512]{0:T(512)}, u32[]{:S(2)}) copy-start(f32[512]{0:T(512)} %constant.88) | copy-start | bytes 6148
  17.5 0.7 %copy-start.4 = (s32[512]{0:T(512)S(1)}, s32[512]{0:T(512)}, u32[]{:S(2)}) copy-start(s32[512]{0:T(512)} %constant.79.clone) | copy-start | bytes 6148
  28.6 15.7 %copy-start = (bf16[384,128]{1,0:T(8,128)(2,1)S(1)}, bf16[384,128]{1,0:T(8,128)(2,1)}, u32[]{:S(2)}) copy-start(bf16[384,128]{1,0:T(8,128)(2,1)} %constant.80.clone.fore_ref) | copy-start | bytes 294916
  28.6 15.7 %copy-start.1 = (bf16[384,128]{1,0:T(8,128)(2,1)S(1)}, bf16[384,128]{1,0:T(8,128)(2,1)}, u32[]{:S(2)}) copy-start(bf16[384,128]{1,0:T(8,128)(2,1)} %constant.81.clone.back_ref) | copy-start | bytes 294916
  28.6 15.7 %copy-start.2 = (f32[2,16,128]{2,1,0:T(8,128)S(1)}, f32[2,16,128]{2,1,0:T(8,128)}, u32[]{:S(2)}) copy-start(f32[2,16,128]{2,1,0:T(8,128)} %constant.82.clone.turn_ref) | copy-start | bytes 49156

commit v7 on v5

--- a/solution.py
+++ b/solution.py
@@ -185,11 +185,10 @@
     total = None
     for c in range(chunks):
         lines = decoded(codes_ref[c * size : (c + 1) * size]).reshape(size * freqs, lanes)
-        line_high, line_low = split(lines)
+        line_high = lines.astype(jnp.bfloat16)
         table = table_ref[:, c * size * freqs : (c + 1) * size * freqs]
         both = jnp.dot(table, line_high, preferred_element_type=jnp.float32)
         both = both[: 2 * rows] + both[2 * rows :]
-        both = both + jnp.dot(table[: 2 * rows], line_low, preferred_element_type=jnp.float32)
         total = both if total is None else total + both
     out_ref[...] = total[:rows, :width] + other_half(total[rows:])[:, :width]
 

time: 60.8 us -> 60.7 us (level)
  no operation moved by 1% of the time
where the time goes in v7:
time: 60.7 us; the launch traced here: 60.4 us
  blocking collectives  29.8 us (49%)
  starting transfers between devices  13.3 us (22%)
  waiting for transfers between devices  10.1 us (17%)
  Pallas kernels  4.36 us (7%)
  local copies, waits for them, and re-layouts  1.56 us (3%)
  other arithmetic  1.04 us (2%)
    all_to_all x1, blocking collectives, body(): gathered = lax.all_to_all(stacked, ('core', 'high'), 0, 0, tiled=True)  15.7 us
    all_to_all x1, blocking collectives, body(): returned = lax.all_to_all(lines, ('x', 'z', 'low'), 0, 0, tiled=True)  14.2 us
    all_to_all x1, starting transfers between devices, body(): lax.all_to_all(spectra.reshape(owners, 2 * freq_local, lanes), ('z', 'x',...  13.3 us
    all_to_all x1, waiting for transfers between devices, body(): lax.all_to_all(spectra.reshape(owners, 2 * freq_local, lanes), ('z', 'x',...  10.1 us
    pallas_call x1, Pallas kernels, body(): pl.pallas_call(lag_kernel, in_specs=[HBM] * 3, out_specs=VMEM, compiler_p...  2.57 us
  transfers between devices with their start and end apart: 1, of which 1 were waited for; matrix products, arithmetic and copies ran while one was open for 2% of the time, Pallas kernels for 0%

profile of v7, /device:TPU:8, one launch (start us, length us, event | category | flops | bytes accessed | tf_op | source)
XLA Modules:
  0.0 60.4 jit_solution(13506835730170808776)
XLA Ops:
  0.0 2.6 %shard_map.91 = bf16[1024,128]{1,0:T(8,128)(2,1)} custom-call(bf16[1024,512]{1,0:T(8,128)(2,1)} %constant.78.clone.table_hbm, bf16[64,1024]{1,0:T(8,128)(2,1)} %bitcast.16, bf16[64,1024]{1,0:T(8,128)(2,1)} %bitcast.17), custom_call_target="tpu_custom_call" | custom-call | tf_op jit(solution)/shard_map/pallas_call | solution.py:212
  2.6 0.0 copy-start.3
  2.6 13.3 %all-to-all-start = ((bf16[32,32,128]{2,1,0:T(8,128)(2,1)}), bf16[32,32,128]{2,1,0:T(8,128)(2,1)S(1)}, u32[]{:S(2)}, u32[]{:S(2)}) async-start(bf16[32,32,128]{2,1,0:T(8,128)(2,1)} %bitcast.2), calls=%async_computation | async-start | bytes 524288 | tf_op jit(solution)/shard_map/all_to_all | solution.py:233
  15.9 0.1 fusion.11
  16.0 0.0 copy-done.3
  16.0 0.2 reshape.192
  16.2 0.0 copy-start.7
  16.2 0.2 copy.14
  16.4 0.5 copy-done.7
  16.9 0.4 select_reduce_fusion
  17.3 0.1 pad_maximum_fusion
  17.4 0.0 copy-start.6
  17.4 0.1 maximum_bitcast_fusion
  17.5 0.0 copy-start.5
  17.5 0.0 copy-start.4
  17.5 0.6 copy-done.6
  18.1 0.1 copy-done.5
  18.2 0.0 copy-done.4
  18.2 0.3 cosine_multiply_fusion
  18.6 10.1 %all-to-all-done = bf16[32,32,128]{2,1,0:T(8,128)(2,1)S(1)} async-done(((bf16[32,32,128]{2,1,0:T(8,128)(2,1)}), bf16[32,32,128]{2,1,0:T(8,128)(2,1)S(1)}, u32[]{:S(2)}, u32[]{:S(2)}) %all-to-all-start) | async-done | bytes 262176 | tf_op jit(solution)/shard_map/all_to_all | solution.py:233
  28.7 0.2 shard_map.92
  28.9 0.0 copy-start
  28.9 0.0 copy-start.1
  28.9 0.0 copy-start.2
  29.0 15.7 %all_to_all.15.lines_ref = bf16[16,1,32,128]{3,2,1,0:T(8,128)(2,1)S(1)} all-to-all(bf16[16,1,32,128]{3,2,1,0:T(8,128)(2,1)S(1)} %shard_map.92), channel_id=1, replica_groups=mesh['z'=8,'x'=4,'high'=8,'low'=1,'core'=2] {'core','high'}, dimensions={0} | all-to-all | bytes 262144 | tf_op jit(solution)/shard_map/all_to_all | solution.py:285
  44.6 0.0 copy-done
  44.6 0.0 copy-done.1
  44.6 0.0 copy-done.2
  44.6 0.7 %shard_map.93 = bf16[32,16,128]{2,1,0:T(8,128)(2,1)S(1)} custom-call(bf16[16,1,32,128]{3,2,1,0:T(8,128)(2,1)S(1)} %all_to_all.15.lines_ref, f32[256,128]{1,0:T(8,128)S(1)} %bitcast.14, bf16[384,128]{1,0:T(8,128)(2,1)S(1)} %copy-done, bf16[384,128]{1,0:T(8,128)(2,1)S(1)} %copy-done.1, f32[2,16,128]{2,1,0:T(8,128)S(1)} %copy-done.2, ...), custom_call_target="tpu_custom_call" | custom-call | tf_op jit(solution)/shard_map/pallas_call | solution.py:286
  45.3 14.2 %all_to_all.16.codes_ref = bf16[32,16,128]{2,1,0:T(8,128)(2,1)S(1)} all-to-all(bf16[32,16,128]{2,1,0:T(8,128)(2,1)S(1)} %shard_map.93), channel_id=1, replica_groups=mesh['z'=8,'x'=4,'high'=8,'low'=1,'core'=2] {'x','z','low'}, dimensions={0} | all-to-all | bytes 262144 | tf_op jit(solution)/shard_map/all_to_all | solution.py:301
  59.5 0.9 %shard_map.94 = f32[32,64]{1,0:T(8,128)} custom-call(bf16[32,16,128]{2,1,0:T(8,128)(2,1)S(1)} %all_to_all.16.codes_ref, bf16[128,512]{1,0:T(8,128)(2,1)S(1)} %pad_maximum_fusion.2.table_ref), custom_call_target="tpu_custom_call" | custom-call | tf_op jit(solution)/shard_map/pallas_call | solution.py:304
  (5 shorter events, 0.0 us)
Async XLA Ops:
  2.6 13.4 %copy-start.3 = (s32[16,1024]{1,0:T(8,128)S(1)}, s32[16,1024]{1,0:T(8,128)}, u32[]{:S(2)}) copy-start(s32[16,1024]{1,0:T(8,128)} %param.11) | copy-start | bytes 196612
  2.6 26.1 %all-to-all-start = ((bf16[32,32,128]{2,1,0:T(8,128)(2,1)}), bf16[32,32,128]{2,1,0:T(8,128)(2,1)S(1)}, u32[]{:S(2)}, u32[]{:S(2)}) async-start(bf16[32,32,128]{2,1,0:T(8,128)(2,1)} %bitcast.2), calls=%async_computation | async-start | bytes 524288 | tf_op jit(solution)/shard_map/all_to_all | solution.py:233
  16.2 0.7 %copy-start.7 = (f32[8]{0:T(128)S(1)}, f32[8]{0:T(128)}, u32[]{:S(2)}) copy-start(f32[8]{0:T(128)} %param.12) | copy-start | bytes 100
  17.4 0.7 %copy-start.6 = (f32[512]{0:T(512)S(1)}, f32[512]{0:T(512)}, u32[]{:S(2)}) copy-start(f32[512]{0:T(512)} %constant.89) | copy-start | bytes 6148
  17.5 0.7 %copy-start.5 = (f32[512]{0:T(512)S(1)}, f32[512]{0:T(512)}, u32[]{:S(2)}) copy-start(f32[512]{0:T(512)} %constant.88) | copy-start | bytes 6148
  17.5 0.7 %copy-start.4 = (s32[512]{0:T(512)S(1)}, s32[512]{0:T(512)}, u32[]{:S(2)}) copy-start(s32[512]{0:T(512)} %constant.79.clone) | copy-start | bytes 6148
  28.9 15.7 %copy-start = (bf16[384,128]{1,0:T(8,128)(2,1)S(1)}, bf16[384,128]{1,0:T(8,128)(2,1)}, u32[]{:S(2)}) copy-start(bf16[384,128]{1,0:T(8,128)(2,1)} %constant.80.clone.fore_ref) | copy-start | bytes 294916
  28.9 15.7 %copy-start.1 = (bf16[384,128]{1,0:T(8,128)(2,1)S(1)}, bf16[384,128]{1,0:T(8,128)(2,1)}, u32[]{:S(2)}) copy-start(bf16[384,128]{1,0:T(8,128)(2,1)} %constant.81.clone.back_ref) | copy-start | bytes 294916
  28.9 15.7 %copy-start.2 = (f32[2,16,128]{2,1,0:T(8,128)S(1)}, f32[2,16,128]{2,1,0:T(8,128)}, u32[]{:S(2)}) copy-start(f32[2,16,128]{2,1,0:T(8,128)} %constant.82.clone.turn_ref) | copy-start | bytes 49156

commit v8 on v5

--- a/solution.py
+++ b/solution.py
@@ -314,7 +314,7 @@
 
 def solution(mesh):
     days, tiles = mesh.devices.shape
-    split = Mesh(mesh.devices.reshape(days // 4, 4, tiles // 2, 1, 2), AXES)
+    split = Mesh(mesh.devices.reshape(days // 4, 4, tiles // 4, 2, 2), AXES)
     day, tile = ("z", "x"), ("high", "low", "core")
     return jax.shard_map(
         body,

time: 60.8 us -> 61.8 us (1.016)
  starting transfers between devices: 13.3 us -> 14.8 us
    all_to_all x1, starting transfers between devices: 13.3 us -> 14.8 us  [body(): lax.all_to_all(spectra.reshape(owners, 2 * freq_local, lanes), ('z', 'x',...]
    all_to_all x1, blocking collectives: 15.7 us -> 14.5 us  [body(): gathered = lax.all_to_all(stacked, ('core', 'high'), 0, 0, tiled=True)]
    all_to_all x1, blocking collectives: 14.2 us -> 15.2 us  [body(): returned = lax.all_to_all(lines, ('x', 'z', 'low'), 0, 0, tiled=True)]
where the time goes in v8:
time: 61.8 us; the launch traced here: 61.5 us
  blocking collectives  29.7 us (48%)
  starting transfers between devices  14.8 us (24%)
  waiting for transfers between devices  10.1 us (16%)
  Pallas kernels  4.37 us (7%)
  local copies, waits for them, and re-layouts  1.47 us (2%)
  other arithmetic  0.95 us (2%)
    all_to_all x1, blocking collectives, body(): returned = lax.all_to_all(lines, ('x', 'z', 'low'), 0, 0, tiled=True)  15.2 us
    all_to_all x1, starting transfers between devices, body(): lax.all_to_all(spectra.reshape(owners, 2 * freq_local, lanes), ('z', 'x',...  14.8 us
    all_to_all x1, blocking collectives, body(): gathered = lax.all_to_all(stacked, ('core', 'high'), 0, 0, tiled=True)  14.5 us
    all_to_all x1, waiting for transfers between devices, body(): lax.all_to_all(spectra.reshape(owners, 2 * freq_local, lanes), ('z', 'x',...  10.1 us
    pallas_call x1, Pallas kernels, body(): pl.pallas_call(lag_kernel, in_specs=[HBM] * 3, out_specs=VMEM, compiler_p...  2.59 us
  transfers between devices with their start and end apart: 1, of which 1 were waited for; matrix products, arithmetic and copies ran while one was open for 2% of the time, Pallas kernels for 0%

profile of v8, /device:TPU:8, one launch (start us, length us, event | category | flops | bytes accessed | tf_op | source)
XLA Modules:
  0.0 61.5 jit_solution(6881937983286158717)
XLA Ops:
  0.0 0.0 copy-start
  0.0 2.6 %shard_map.91 = bf16[1024,128]{1,0:T(8,128)(2,1)} custom-call(bf16[1024,512]{1,0:T(8,128)(2,1)} %constant.81.clone.table_hbm, bf16[64,1024]{1,0:T(8,128)(2,1)} %bitcast.18, bf16[64,1024]{1,0:T(8,128)(2,1)} %bitcast.19), custom_call_target="tpu_custom_call" | custom-call | tf_op jit(solution)/shard_map/pallas_call | solution.py:213
  2.6 14.8 %all-to-all-start = ((bf16[64,16,128]{2,1,0:T(8,128)(2,1)}), bf16[64,16,128]{2,1,0:T(8,128)(2,1)S(1)}, u32[]{:S(2)}, u32[]{:S(2)}) async-start(bf16[64,16,128]{2,1,0:T(8,128)(2,1)} %bitcast.2), calls=%async_computation | async-start | bytes 524288 | tf_op jit(solution)/shard_map/all_to_all | solution.py:234
  17.4 0.0 copy-done
  17.4 0.1 reshape.59
  17.6 0.0 copy-start.7
  17.6 0.1 copy.15
  17.7 0.5 copy-done.7
  18.2 0.2 select_reduce_fusion
  18.5 0.1 maximum_bitcast_fusion.gains_ref
  18.6 0.1 iota_add_fusion
  18.7 0.1 fusion.11
  18.8 0.1 maximum_bitcast_fusion.1
  18.8 0.0 copy-start.6
  18.8 0.0 copy-start.5
  18.9 0.0 copy-start.4
  18.9 0.6 %copy-done.6 = f32[512]{0:T(512)S(1)} copy-done((f32[512]{0:T(512)S(1)}, f32[512]{0:T(512)}, u32[]{:S(2)}) %copy-start.6) | copy-done | bytes 2072
  19.5 0.0 copy-done.5
  19.5 0.0 copy-done.4
  19.5 0.3 cosine_multiply_fusion
  19.9 10.1 %all-to-all-done = bf16[64,16,128]{2,1,0:T(8,128)(2,1)S(1)} async-done(((bf16[64,16,128]{2,1,0:T(8,128)(2,1)}), bf16[64,16,128]{2,1,0:T(8,128)(2,1)S(1)}, u32[]{:S(2)}, u32[]{:S(2)}) %all-to-all-start) | async-done | bytes 262176 | tf_op jit(solution)/shard_map/all_to_all | solution.py:234
  30.0 0.0 copy-start.2
  30.0 0.2 shard_map.92
  30.2 0.0 copy-start.1
  30.2 0.0 copy-start.3
  30.2 14.5 %all_to_all.15.lines_ref = bf16[8,2,16,128]{3,2,1,0:T(8,128)(2,1)S(1)} all-to-all(bf16[8,2,16,128]{3,2,1,0:T(8,128)(2,1)S(1)} %shard_map.92), channel_id=1, replica_groups=mesh['z'=8,'x'=4,'high'=4,'low'=2,'core'=2] {'core','high'}, dimensions={0} | all-to-all | bytes 131072 | tf_op jit(solution)/shard_map/all_to_all | solution.py:286
  44.8 0.0 copy-done.2
  44.8 0.0 copy-done.1
  44.8 0.0 copy-done.3
  44.8 0.7 %shard_map.93 = bf16[64,8,128]{2,1,0:T(8,128)(2,1)S(1)} custom-call(bf16[8,2,16,128]{3,2,1,0:T(8,128)(2,1)S(1)} %all_to_all.15.lines_ref, f32[128,128]{1,0:T(8,128)S(1)} %maximum_bitcast_fusion.gains_ref, bf16[384,128]{1,0:T(8,128)(2,1)S(1)} %copy-done.1, bf16[384,128]{1,0:T(8,128)(2,1)S(1)} %copy-done.2, f32[2,16,128]{2,1,0:T(8,128)S(1)} %copy-done.3, ...), custom_call_target="tpu_custom_call" | custom-call | tf_op jit(solution)/shard_map/pallas_call | solution.py:287
  45.4 15.2 %all_to_all.16.codes_ref = bf16[64,8,128]{2,1,0:T(8,128)(2,1)S(1)} all-to-all(bf16[64,8,128]{2,1,0:T(8,128)(2,1)S(1)} %shard_map.93), channel_id=1, replica_groups=mesh['z'=8,'x'=4,'high'=4,'low'=2,'core'=2] {'x','z','low'}, dimensions={0} | all-to-all | bytes 262144 | tf_op jit(solution)/shard_map/all_to_all | solution.py:302
  60.6 0.9 %shard_map.94 = f32[32,64]{1,0:T(8,128)} custom-call(bf16[64,8,128]{2,1,0:T(8,128)(2,1)S(1)} %all_to_all.16.codes_ref, bf16[128,512]{1,0:T(8,128)(2,1)S(1)} %pad_maximum_fusion.1.table_ref), custom_call_target="tpu_custom_call" | custom-call | tf_op jit(solution)/shard_map/pallas_call | solution.py:305
  (6 shorter events, 0.1 us)
Async XLA Ops:
  0.0 17.4 %copy-start = (s32[16,1024]{1,0:T(8,128)S(1)}, s32[16,1024]{1,0:T(8,128)}, u32[]{:S(2)}) copy-start(s32[16,1024]{1,0:T(8,128)} %param.11) | copy-start | bytes 196612
  2.6 27.4 %all-to-all-start = ((bf16[64,16,128]{2,1,0:T(8,128)(2,1)}), bf16[64,16,128]{2,1,0:T(8,128)(2,1)S(1)}, u32[]{:S(2)}, u32[]{:S(2)}) async-start(bf16[64,16,128]{2,1,0:T(8,128)(2,1)} %bitcast.2), calls=%async_computation | async-start | bytes 524288 | tf_op jit(solution)/shard_map/all_to_all | solution.py:234
  17.6 0.7 %copy-start.7 = (f32[8]{0:T(128)S(1)}, f32[8]{0:T(128)}, u32[]{:S(2)}) copy-start(f32[8]{0:T(128)} %param.12) | copy-start | bytes 100
  18.8 0.7 %copy-start.6 = (f32[512]{0:T(512)S(1)}, f32[512]{0:T(512)}, u32[]{:S(2)}) copy-start(f32[512]{0:T(512)} %constant.92) | copy-start | bytes 6148
  18.8 0.7 %copy-start.5 = (f32[512]{0:T(512)S(1)}, f32[512]{0:T(512)}, u32[]{:S(2)}) copy-start(f32[512]{0:T(512)} %constant.91) | copy-start | bytes 6148
  18.9 0.7 %copy-start.4 = (s32[512]{0:T(512)S(1)}, s32[512]{0:T(512)}, u32[]{:S(2)}) copy-start(s32[512]{0:T(512)} %constant.82.clone) | copy-start | bytes 6148
  30.0 14.8 %copy-start.2 = (bf16[384,128]{1,0:T(8,128)(2,1)S(1)}, bf16[384,128]{1,0:T(8,128)(2,1)}, u32[]{:S(2)}) copy-start(bf16[384,128]{1,0:T(8,128)(2,1)} %constant.84.clone.back_ref) | copy-start | bytes 294916
  30.2 14.6 %copy-start.1 = (bf16[384,128]{1,0:T(8,128)(2,1)S(1)}, bf16[384,128]{1,0:T(8,128)(2,1)}, u32[]{:S(2)}) copy-start(bf16[384,128]{1,0:T(8,128)(2,1)} %constant.83.clone.fore_ref) | copy-start | bytes 294916
  30.2 14.6 %copy-start.3 = (f32[2,16,128]{2,1,0:T(8,128)S(1)}, f32[2,16,128]{2,1,0:T(8,128)}, u32[]{:S(2)}) copy-start(f32[2,16,128]{2,1,0:T(8,128)} %constant.85.clone.turn_ref) | copy-start | bytes 49156

commit v9 on v5

--- a/solution.py
+++ b/solution.py
@@ -151,7 +151,7 @@
     for block in range(blocks):
         high, pair, core = block // (2 * pairs), block // 2 % pairs, block % 2
         highs = peers // 2
-        peer, other = core * highs + high, core * highs + (high + highs // 2) % highs
+        peer, other = 2 * high + core, 2 * ((high + highs // 2) % highs) + core
         data.append(value[peer, pair, :half] + value[other, pair, half:])
     inner = [four(*(data[4 * a + b] for a in range(4))) for b in range(4)]
     for c in range(4):
@@ -283,7 +283,7 @@
             halves(np.sin(turn_angle), -np.sin(turn_angle)),
         ]
     )
-    gathered = lax.all_to_all(stacked, ("core", "high"), 0, 0, tiled=True)
+    gathered = lax.all_to_all(stacked, ("high", "core"), 0, 0, tiled=True)
     lines = pl.pallas_call(
         filter_kernel,
         in_specs=[VMEM] * 6,

time: 60.8 us -> 61 us (level)
  the two profiles are of different devices: /device:TPU:8 before, /device:TPU:1 now
where the time goes in v9:
time: 61 us; the launch traced here: 60.6 us
  blocking collectives  31 us (51%)
  starting transfers between devices  13.9 us (23%)
  waiting for transfers between devices  8.63 us (14%)
  Pallas kernels  4.38 us (7%)
  local copies, waits for them, and re-layouts  1.56 us (3%)
  other arithmetic  1.04 us (2%)
    all_to_all x1, blocking collectives, body(): gathered = lax.all_to_all(stacked, ('high', 'core'), 0, 0, tiled=True)  18.4 us
    all_to_all x1, starting transfers between devices, body(): lax.all_to_all(spectra.reshape(owners, 2 * freq_local, lanes), ('z', 'x',...  13.9 us
    all_to_all x1, blocking collectives, body(): returned = lax.all_to_all(lines, ('x', 'z', 'low'), 0, 0, tiled=True)  12.6 us
    all_to_all x1, waiting for transfers between devices, body(): lax.all_to_all(spectra.reshape(owners, 2 * freq_local, lanes), ('z', 'x',...  8.63 us
    pallas_call x1, Pallas kernels, body(): pl.pallas_call(lag_kernel, in_specs=[HBM] * 3, out_specs=VMEM, compiler_p...  2.57 us
  transfers between devices with their start and end apart: 1, of which 1 were waited for; matrix products, arithmetic and copies ran while one was open for 2% of the time, Pallas kernels for 0%

profile of v9, /device:TPU:1, one launch (start us, length us, event | category | flops | bytes accessed | tf_op | source)
XLA Modules:
  0.0 60.6 jit_solution(4322513898550431173)
XLA Ops:
  0.0 2.6 %shard_map.91 = bf16[1024,128]{1,0:T(8,128)(2,1)} custom-call(bf16[1024,512]{1,0:T(8,128)(2,1)} %constant.78.clone.table_hbm, bf16[64,1024]{1,0:T(8,128)(2,1)} %bitcast.16, bf16[64,1024]{1,0:T(8,128)(2,1)} %bitcast.17), custom_call_target="tpu_custom_call" | custom-call | tf_op jit(solution)/shard_map/pallas_call | solution.py:213
  2.6 0.0 copy-start.3
  2.6 13.9 %all-to-all-start = ((bf16[32,32,128]{2,1,0:T(8,128)(2,1)}), bf16[32,32,128]{2,1,0:T(8,128)(2,1)S(1)}, u32[]{:S(2)}, u32[]{:S(2)}) async-start(bf16[32,32,128]{2,1,0:T(8,128)(2,1)} %bitcast.2), calls=%async_computation | async-start | bytes 524288 | tf_op jit(solution)/shard_map/all_to_all | solution.py:234
  16.5 0.1 fusion.11
  16.5 0.0 copy-done.3
  16.5 0.2 reshape.192
  16.8 0.0 copy-start.7
  16.8 0.2 copy.14
  17.0 0.5 copy-done.7
  17.4 0.4 select_reduce_fusion
  17.8 0.1 pad_maximum_fusion
  17.9 0.0 copy-start.6
  18.0 0.1 maximum_bitcast_fusion
  18.0 0.0 copy-start.5
  18.0 0.0 copy-start.4
  18.1 0.6 copy-done.6
  18.6 0.1 copy-done.5
  18.7 0.0 copy-done.4
  18.7 0.3 cosine_multiply_fusion
  19.1 8.6 %all-to-all-done = bf16[32,32,128]{2,1,0:T(8,128)(2,1)S(1)} async-done(((bf16[32,32,128]{2,1,0:T(8,128)(2,1)}), bf16[32,32,128]{2,1,0:T(8,128)(2,1)S(1)}, u32[]{:S(2)}, u32[]{:S(2)}) %all-to-all-start) | async-done | bytes 262176 | tf_op jit(solution)/shard_map/all_to_all | solution.py:234
  27.8 0.2 shard_map.92
  28.0 0.0 copy-start
  28.0 0.0 copy-start.1
  28.0 0.0 copy-start.2
  28.0 18.4 %all_to_all.15.lines_ref = bf16[16,1,32,128]{3,2,1,0:T(8,128)(2,1)S(1)} all-to-all(bf16[16,1,32,128]{3,2,1,0:T(8,128)(2,1)S(1)} %shard_map.92), channel_id=1, replica_groups=mesh['z'=8,'x'=4,'high'=8,'low'=1,'core'=2] {'high','core'}, dimensions={0} | all-to-all | bytes 262144 | tf_op jit(solution)/shard_map/all_to_all | solution.py:286
  46.4 0.0 copy-done
  46.4 0.0 copy-done.1
  46.4 0.0 copy-done.2
  46.4 0.7 %shard_map.93 = bf16[32,16,128]{2,1,0:T(8,128)(2,1)S(1)} custom-call(bf16[16,1,32,128]{3,2,1,0:T(8,128)(2,1)S(1)} %all_to_all.15.lines_ref, f32[256,128]{1,0:T(8,128)S(1)} %bitcast.14, bf16[384,128]{1,0:T(8,128)(2,1)S(1)} %copy-done, bf16[384,128]{1,0:T(8,128)(2,1)S(1)} %copy-done.1, f32[2,16,128]{2,1,0:T(8,128)S(1)} %copy-done.2, ...), custom_call_target="tpu_custom_call" | custom-call | tf_op jit(solution)/shard_map/pallas_call | solution.py:287
  47.1 12.6 %all_to_all.16.codes_ref = bf16[32,16,128]{2,1,0:T(8,128)(2,1)S(1)} all-to-all(bf16[32,16,128]{2,1,0:T(8,128)(2,1)S(1)} %shard_map.93), channel_id=1, replica_groups=mesh['z'=8,'x'=4,'high'=8,'low'=1,'core'=2] {'x','z','low'}, dimensions={0} | all-to-all | bytes 262144 | tf_op jit(solution)/shard_map/all_to_all | solution.py:302
  59.7 0.9 %shard_map.94 = f32[32,64]{1,0:T(8,128)} custom-call(bf16[32,16,128]{2,1,0:T(8,128)(2,1)S(1)} %all_to_all.16.codes_ref, bf16[128,512]{1,0:T(8,128)(2,1)S(1)} %pad_maximum_fusion.2.table_ref), custom_call_target="tpu_custom_call" | custom-call | tf_op jit(solution)/shard_map/pallas_call | solution.py:305
  (5 shorter events, 0.0 us)
Async XLA Ops:
  2.6 14.0 %copy-start.3 = (s32[16,1024]{1,0:T(8,128)S(1)}, s32[16,1024]{1,0:T(8,128)}, u32[]{:S(2)}) copy-start(s32[16,1024]{1,0:T(8,128)} %param.11) | copy-start | bytes 196612
  2.6 25.2 %all-to-all-start = ((bf16[32,32,128]{2,1,0:T(8,128)(2,1)}), bf16[32,32,128]{2,1,0:T(8,128)(2,1)S(1)}, u32[]{:S(2)}, u32[]{:S(2)}) async-start(bf16[32,32,128]{2,1,0:T(8,128)(2,1)} %bitcast.2), calls=%async_computation | async-start | bytes 524288 | tf_op jit(solution)/shard_map/all_to_all | solution.py:234
  16.8 0.7 %copy-start.7 = (f32[8]{0:T(128)S(1)}, f32[8]{0:T(128)}, u32[]{:S(2)}) copy-start(f32[8]{0:T(128)} %param.12) | copy-start | bytes 100
  17.9 0.7 %copy-start.6 = (f32[512]{0:T(512)S(1)}, f32[512]{0:T(512)}, u32[]{:S(2)}) copy-start(f32[512]{0:T(512)} %constant.89) | copy-start | bytes 6148
  18.0 0.7 %copy-start.5 = (f32[512]{0:T(512)S(1)}, f32[512]{0:T(512)}, u32[]{:S(2)}) copy-start(f32[512]{0:T(512)} %constant.88) | copy-start | bytes 6148
  18.0 0.7 %copy-start.4 = (s32[512]{0:T(512)S(1)}, s32[512]{0:T(512)}, u32[]{:S(2)}) copy-start(s32[512]{0:T(512)} %constant.79.clone) | copy-start | bytes 6148
  28.0 18.4 %copy-start = (bf16[384,128]{1,0:T(8,128)(2,1)S(1)}, bf16[384,128]{1,0:T(8,128)(2,1)}, u32[]{:S(2)}) copy-start(bf16[384,128]{1,0:T(8,128)(2,1)} %constant.80.clone.fore_ref) | copy-start | bytes 294916
  28.0 18.4 %copy-start.1 = (bf16[384,128]{1,0:T(8,128)(2,1)S(1)}, bf16[384,128]{1,0:T(8,128)(2,1)}, u32[]{:S(2)}) copy-start(bf16[384,128]{1,0:T(8,128)(2,1)} %constant.81.clone.back_ref) | copy-start | bytes 294916
  28.0 18.4 %copy-start.2 = (f32[2,16,128]{2,1,0:T(8,128)S(1)}, f32[2,16,128]{2,1,0:T(8,128)}, u32[]{:S(2)}) copy-start(f32[2,16,128]{2,1,0:T(8,128)} %constant.82.clone.turn_ref) | copy-start | bytes 49156
